TPU v7x, 32 devices: a whole 2x2x4 slice. The times are simulated.
32 devices in a mesh: dp: 8 (over y, x, core), expert: 4 (over z).
Axes of the slice: x: 2, y: 2, z: 4, core: 2. Of those that a mesh axis runs over, the one named last changes fastest.
Arguments:
- tokens: bfloat16 [2, 8192, 512], P(None, ('dp', 'expert')), may hold values from -6 to 6
- image_ids: int32 [2, 8192], P(None, ('dp', 'expert')), may hold values from 0 to 41, never falling along the last dimension, each value on 1 to 197 neighbouring positions
- routes: int32 [2, 8192, 2], P(None, ('dp', 'expert')), may hold values from 0 to 7, all different within a row; in each aligned block of 256 rows (0 to 255, 256 to 511, ..., all dimensions but the last counted through in order) at most 128 rows name the same one
- qkv_weight: bfloat16 [3, 512, 512], P(None, ('dp', 'expert')), may hold values from -0.375 to 0.375
- out_weight: bfloat16 [512, 512], P(('dp', 'expert')), may hold values from -0.375 to 0.375
- router_weight: bfloat16 [512, 8], P(('dp', 'expert')), may hold values from -0.1875 to 0.1875
- norm_gains: bfloat16 [2, 512], P(None, ('dp', 'expert')), may hold values from 0.5 to 1.5
- norm_biases: bfloat16 [2, 512], P(None, ('dp', 'expert')), may hold values from -2 to 2
- expert_in: bfloat16 [8, 512, 2048], P('expert', 'dp'), may hold values from -0.25 to 0.25
- expert_out: bfloat16 [8, 2048, 512], P('expert', 'dp'), may hold values from -1 to 1
- cotangent: bfloat16 [2, 8192, 512], P(None, ('dp', 'expert')), may hold values from -6 to 6
Outputs:
- block_out: bfloat16 [2, 8192, 512], P(None, ('dp', 'expert'))
- input_grad: bfloat16 [2, 8192, 512], P(None, ('dp', 'expert'))
- qkv_grad: float32 [3, 512, 512], P(None, ('dp', 'expert'))
- out_grad: float32 [512, 512], P(('dp', 'expert'))
- router_grad: float32 [512, 8], P(('dp', 'expert'))
- gains_grad: float32 [2, 512], P(None, ('dp', 'expert'))
- biases_grad: float32 [2, 512], P(None, ('dp', 'expert'))
- expert_in_grad: float32 [8, 512, 2048], P('expert', 'dp')
- expert_out_grad: float32 [8, 2048, 512], P('expert', 'dp')
Inputs may be any that keep to these rules, and one draw needn't show every extreme that they name: `image_ids`: along each micro-batch's rows the numbers never fall and start at 0; each image has 1 to 197 rows, some image exactly 197. `routes`: A row names two different experts. Within one micro-batch, the 256 rows held by one device name any one expert at most 128 times, counting both choices; this most is reached.
All inputs are finite; a program needn't handle non-finite values.
Results may differ from a plain program's by a relative error of at most 0.015.
The roundings to bfloat16 on the way count: a program that leaves them out, or rounds other values in their place, can miss the bound.
Values may be sent and summed in bfloat16 or wider, within the bound.
A program may use at most 192 MiB of HBM per device.

v0:
```python
import functools
import math

import jax
import jax.numpy as jnp
from jax import lax
from jax.experimental import pallas as pl
from jax.experimental.pallas import tpu as pltpu
from jax.sharding import PartitionSpec as P

D = 512
HEADS = 8
HEAD_DIM = 64
FF = 2048
TOP = 2
IMG = 197
MICRO = 2


neg_big = -1e30
norm_eps = 1e-06
highest = lax.Precision.HIGHEST


def padded(cells, sides, width):
    for axis, dim in sides:
        count = lax.axis_size(axis)
        ends = count - 1
        head = lax.slice_in_dim(cells, 0, width, axis=dim)
        tail = lax.slice_in_dim(cells, cells.shape[dim] - width, cells.shape[dim], axis=dim)
        cells = jnp.concatenate(
            [
                lax.ppermute(tail, axis, [(i, (i + 1) % count) for i in range(ends)]),
                cells,
                lax.ppermute(head, axis, [((i + 1) % count, i) for i in range(ends)]),
            ],
            axis=dim,
        )
    return cells


def layer_norm(values, gain_row, bias_row):
    centre = jnp.mean(values, axis=-1, keepdims=True)
    offset = values - centre
    spread = jnp.mean(offset * offset, axis=-1, keepdims=True)
    return offset * lax.rsqrt(spread + norm_eps) * gain_row + bias_row


def tanh_gelu(values):
    return jax.nn.gelu(values, approximate=True)


def fetch_dense(qkv_weight, out_weight, router_weight, norm_gains, norm_biases):
    rows, experts = router_weight.shape
    small = jnp.concatenate([router_weight, norm_gains.T, norm_biases.T], axis=1)
    small = jnp.pad(small, ((0, 0), (0, D - experts - 4)))
    packed = jnp.concatenate([qkv_weight, out_weight[None], small[None]], axis=0)
    full = lax.all_gather(packed, ("dp", "expert"), axis=1, tiled=True)
    return (
        full[:3],
        full[3],
        full[4][:, :experts],
        full[4][:, experts : experts + 2].T,
        full[4][:, experts + 2 : experts + 4].T,
    )


def fetch_experts(expert_in, expert_out):
    return (
        lax.all_gather(expert_in, "dp", axis=1, tiled=True),
        lax.all_gather(expert_out, "dp", axis=1, tiled=True),
    )


def plan_routes(route_ids, shard_experts):
    row_count = route_ids.shape[0]
    experts = shard_experts * lax.axis_size("expert")
    devices = lax.axis_size(("dp", "expert"))
    slot_count = 2 * TOP * row_count // experts
    capacity = 5 * TOP * row_count * devices // (4 * experts)
    labels = lax.broadcasted_iota(jnp.int32, (1, experts), 1)
    first_hot = (route_ids[:, 0:1] == labels).astype(jnp.int32)
    second_hot = (route_ids[:, 1:2] == labels).astype(jnp.int32)
    counts = jnp.stack([jnp.sum(first_hot, axis=0), jnp.sum(second_hot, axis=0)])
    all_counts = lax.all_gather(counts[None], ("dp", "expert"), axis=0, tiled=True)
    earlier = (
        lax.broadcasted_iota(jnp.int32, (devices, 1, 1), 0) < lax.axis_index(("dp", "expert"))
    ).astype(jnp.int32)
    before = jnp.sum(all_counts * earlier, axis=0)
    total_first = jnp.sum(all_counts[:, 0, :], axis=0)
    row_before = (
        lax.broadcasted_iota(jnp.int32, (row_count, row_count), 0)
        > lax.broadcasted_iota(jnp.int32, (row_count, row_count), 1)
    ).astype(jnp.bfloat16)

    def rank_of(hot):
        ahead = jnp.dot(row_before, hot.astype(jnp.bfloat16), preferred_element_type=jnp.float32)
        return jnp.sum(ahead.astype(jnp.int32) * hot, axis=1)

    rank_first = rank_of(first_hot)
    rank_second = rank_of(second_hot)
    place_first = jnp.sum(first_hot * before[0][None, :], axis=1) + rank_first
    place_second = jnp.sum(second_hot * (total_first + before[1])[None, :], axis=1) + rank_second
    kept_mask = jnp.stack([place_first < capacity, place_second < capacity], axis=1)
    slot_second = jnp.sum(second_hot * counts[0][None, :], axis=1) + rank_second
    flat_index = jnp.stack(
        [route_ids[:, 0] * slot_count + rank_first, route_ids[:, 1] * slot_count + slot_second],
        axis=1,
    )
    target = jnp.where(kept_mask, flat_index, experts * slot_count)
    return (first_hot, second_hot, target, kept_mask.astype(jnp.float32))


def fill_slots(row_pairs, target, experts, slot_count):
    feature_count = row_pairs.shape[-1]
    buffer = jnp.zeros((experts * slot_count + 1, feature_count), row_pairs.dtype)
    buffer = buffer.at[target.reshape(-1)].set(row_pairs.reshape(-1, feature_count))
    return buffer[:-1].reshape(experts, 1, slot_count, feature_count)


def read_slots(returned, target):
    feature_count = returned.shape[-1]
    flat_table = jnp.concatenate(
        [returned.reshape(-1, feature_count), jnp.zeros((1, feature_count), returned.dtype)], axis=0
    )
    return flat_table[target]


def run_forward(tokens_f, ids_ext, route_plan, dense_set, expert_set):
    qkv_full, out_full, router_full, gain_pair, bias_pair = dense_set
    expert_up_weight, expert_down_weight = expert_set
    first_hot, second_hot, target, kept_mask = route_plan
    row_count = tokens_f.shape[0]
    rim_rows = IMG - 1
    score_scale = 1.0 / math.sqrt(HEAD_DIM)
    experts = router_full.shape[1]
    slot_count = 2 * TOP * row_count // experts
    normed_one = layer_norm(
        tokens_f, gain_pair[0].astype(jnp.float32), bias_pair[0].astype(jnp.float32)
    ).astype(jnp.bfloat16)
    projected = jnp.einsum(
        "rd,cde->cre", normed_one, qkv_full, preferred_element_type=jnp.float32
    ).astype(jnp.bfloat16)
    key_value = padded(projected[1:], ((("dp", "expert"), 1),), rim_rows)
    query_heads = projected[0].reshape(row_count, HEADS, HEAD_DIM)
    key_heads = key_value[0].reshape(-1, HEADS, HEAD_DIM)
    value_heads = key_value[1].reshape(-1, HEADS, HEAD_DIM)
    same_image = ids_ext[rim_rows : rim_rows + row_count][:, None] == ids_ext[None, :]
    scores = (
        jnp.einsum("qhd,khd->hqk", query_heads, key_heads, preferred_element_type=jnp.float32)
        * score_scale
    )
    scores = jnp.where(same_image[None], scores, neg_big)
    top_score = jnp.max(scores, axis=-1, keepdims=True)
    log_total = top_score + jnp.log(jnp.sum(jnp.exp(scores - top_score), axis=-1, keepdims=True))
    att_probs = jnp.exp(scores - log_total)
    att_low = att_probs.astype(jnp.bfloat16)
    mixed_rows = (
        jnp.einsum("hqk,khd->qhd", att_low, value_heads, preferred_element_type=jnp.float32)
        .reshape(row_count, D)
        .astype(jnp.bfloat16)
    )
    residual = tokens_f + jnp.dot(mixed_rows, out_full, preferred_element_type=jnp.float32)
    normed_two = layer_norm(
        residual, gain_pair[1].astype(jnp.float32), bias_pair[1].astype(jnp.float32)
    ).astype(jnp.bfloat16)
    router_probs = jax.nn.softmax(
        jnp.dot(normed_two, router_full, preferred_element_type=jnp.float32), axis=-1
    )
    picked = jnp.stack(
        [jnp.sum(first_hot * router_probs, axis=1), jnp.sum(second_hot * router_probs, axis=1)],
        axis=1,
    )
    gate_values = kept_mask * picked
    outgoing = fill_slots(
        jnp.broadcast_to(normed_two[:, None, :], (row_count, TOP, D)), target, experts, slot_count
    )
    arrived = lax.all_to_all(outgoing, "expert", split_axis=0, concat_axis=1, tiled=True)
    shard_experts = arrived.shape[0]
    collected_token_rows = arrived.reshape(shard_experts, -1, D)
    hidden_pre = jnp.einsum(
        "ycq,yqt->yct", collected_token_rows, expert_up_weight, preferred_element_type=jnp.float32
    )
    hidden_activation = tanh_gelu(hidden_pre).astype(jnp.bfloat16)
    produced = jnp.einsum(
        "nso,nop->nsp", hidden_activation, expert_down_weight, preferred_element_type=jnp.float32
    ).astype(jnp.bfloat16)
    returned = lax.all_to_all(
        produced.reshape(arrived.shape), "expert", split_axis=1, concat_axis=0, tiled=True
    )
    expert_rows = read_slots(returned, target)
    block_value = residual + jnp.sum(
        gate_values[:, :, None] * expert_rows.astype(jnp.float32), axis=1
    )
    return (
        normed_one,
        query_heads,
        key_heads,
        value_heads,
        att_probs,
        att_low,
        mixed_rows,
        residual,
        normed_two,
        router_probs,
        gate_values,
        collected_token_rows,
        hidden_pre,
        hidden_activation,
        expert_rows,
        block_value,
    )


def run_backward(tokens_f, ids_ext, route_plan, dense_set, expert_set, upstream, gradients):
    qkv_full, out_full, router_full, gain_pair, bias_pair = dense_set
    expert_up_weight, expert_down_weight = expert_set
    first_hot, second_hot, target, kept_mask = route_plan
    grad_qkv, grad_out, grad_router, grad_gains, grad_biases, grad_in, grad_expert_out = gradients
    (
        normed_one,
        query_heads,
        key_heads,
        value_heads,
        att_probs,
        att_low,
        mixed_rows,
        residual,
        normed_two,
        router_probs,
        gate_values,
        collected_token_rows,
        hidden_pre,
        hidden_activation,
        expert_rows,
        block_value,
    ) = run_forward(tokens_f, ids_ext, route_plan, dense_set, expert_set)
    row_count = tokens_f.shape[0]
    rim_rows = IMG - 1
    score_scale = 1.0 / math.sqrt(HEAD_DIM)
    experts = router_full.shape[1]
    slot_count = 2 * TOP * row_count // experts
    shard_experts = expert_up_weight.shape[0]
    d_gate = kept_mask * jnp.sum(upstream[:, None, :] * expert_rows.astype(jnp.float32), axis=-1)
    d_sent = (gate_values[:, :, None] * upstream[:, None, :]).astype(jnp.bfloat16)
    d_arrived = lax.all_to_all(
        fill_slots(d_sent, target, experts, slot_count),
        "expert",
        split_axis=0,
        concat_axis=1,
        tiled=True,
    )
    produced_rows_grad = d_arrived.reshape(shard_experts, -1, D)
    activation_grad = jnp.einsum(
        "tkw,tew->tke", produced_rows_grad, expert_down_weight, preferred_element_type=jnp.float32
    )
    grad_expert_out = grad_expert_out + jnp.einsum(
        "meq,mek->mqk", hidden_activation, produced_rows_grad, preferred_element_type=jnp.float32
    )
    gelu_value, gelu_back = jax.vjp(tanh_gelu, hidden_pre)
    preactivation_grad = gelu_back(activation_grad)[0].astype(jnp.bfloat16)
    grad_in = grad_in + jnp.einsum(
        "zjo,zjm->zom", collected_token_rows, preactivation_grad, preferred_element_type=jnp.float32
    )
    d_rows = jnp.einsum(
        "iht,imt->ihm", preactivation_grad, expert_up_weight, preferred_element_type=jnp.float32
    ).astype(jnp.bfloat16)
    d_back = lax.all_to_all(
        d_rows.reshape(d_arrived.shape), "expert", split_axis=1, concat_axis=0, tiled=True
    )
    d_normed_two = jnp.sum(
        kept_mask[:, :, None] * read_slots(d_back, target).astype(jnp.float32), axis=1
    )
    d_probs = first_hot * d_gate[:, 0:1] + second_hot * d_gate[:, 1:2]
    d_logits = router_probs * (d_probs - jnp.sum(router_probs * d_probs, axis=-1, keepdims=True))
    router_wide = router_full.astype(jnp.float32)
    d_normed_two = d_normed_two + jnp.dot(d_logits, router_wide.T, precision=highest)
    grad_router = grad_router + jnp.dot(
        normed_two.astype(jnp.float32).T, d_logits, precision=highest
    )
    norm_value, second_back = jax.vjp(
        layer_norm, residual, gain_pair[1].astype(jnp.float32), bias_pair[1].astype(jnp.float32)
    )
    d_resid_part, d_gain_two, d_bias_two = second_back(d_normed_two)
    d_resid = upstream + d_resid_part
    d_attn = d_resid.astype(jnp.bfloat16)
    grad_out = grad_out + jnp.einsum(
        "rd,re->de", mixed_rows, d_attn, preferred_element_type=jnp.float32
    )
    d_mixed = (
        jnp.einsum("re,de->rd", d_attn, out_full, preferred_element_type=jnp.float32)
        .astype(jnp.bfloat16)
        .reshape(row_count, HEADS, HEAD_DIM)
    )
    d_att = jnp.einsum("qhd,khd->hqk", d_mixed, value_heads, preferred_element_type=jnp.float32)
    d_scores = (att_probs * (d_att - jnp.sum(att_probs * d_att, axis=-1, keepdims=True))).astype(
        jnp.bfloat16
    )
    d_query = (
        (
            jnp.einsum("hqk,khd->qhd", d_scores, key_heads, preferred_element_type=jnp.float32)
            * score_scale
        )
        .astype(jnp.bfloat16)
        .reshape(row_count, D)
    )
    d_key = (
        jnp.einsum("hqk,qhd->khd", d_scores, query_heads, preferred_element_type=jnp.float32)
        * score_scale
    )
    d_value = jnp.einsum("hqk,qhd->khd", att_low, d_mixed, preferred_element_type=jnp.float32)
    d_pair = jnp.stack([d_key.reshape(-1, D), d_value.reshape(-1, D)])
    rim_grads = jnp.concatenate([d_pair[:, :rim_rows], d_pair[:, rim_rows + row_count :]], axis=1)
    beside_all = padded(rim_grads.astype(jnp.bfloat16), ((("dp", "expert"), 1),), rim_rows).astype(
        rim_grads.dtype
    )
    own_part = d_pair[:, rim_rows : rim_rows + row_count]
    from_below = jnp.pad(beside_all[:, :rim_rows], ((0, 0), (0, row_count - rim_rows), (0, 0)))
    from_above = jnp.pad(beside_all[:, 3 * rim_rows :], ((0, 0), (row_count - rim_rows, 0), (0, 0)))
    d_kv = (own_part + from_below + from_above).astype(jnp.bfloat16)
    d_projected = jnp.concatenate([d_query[None], d_kv], axis=0)
    grad_qkv = grad_qkv + jnp.einsum(
        "rd,cre->cde", normed_one, d_projected, preferred_element_type=jnp.float32
    )
    d_normed_one = jnp.einsum(
        "cre,cde->rd", d_projected, qkv_full, preferred_element_type=jnp.float32
    )
    first_value, first_back = jax.vjp(
        layer_norm, tokens_f, gain_pair[0].astype(jnp.float32), bias_pair[0].astype(jnp.float32)
    )
    d_tokens_part, d_gain_one, d_bias_one = first_back(d_normed_one)
    grad_gains = grad_gains + jnp.stack([d_gain_one, d_gain_two])
    grad_biases = grad_biases + jnp.stack([d_bias_one, d_bias_two])
    input_rows = (d_resid + d_tokens_part).astype(jnp.bfloat16)
    return (
        input_rows,
        (grad_qkv, grad_out, grad_router, grad_gains, grad_biases, grad_in, grad_expert_out),
    )


def body(
    tokens,
    image_ids,
    routes,
    qkv_weight,
    out_weight,
    router_weight,
    norm_gains,
    norm_biases,
    expert_in,
    expert_out,
    cotangent,
):
    shard_experts = expert_in.shape[0]
    rim_rows = IMG - 1
    experts = shard_experts * lax.axis_size("expert")
    outputs = []
    saved_state = []
    for batch_index in range(MICRO):
        dense_set = fetch_dense(qkv_weight, out_weight, router_weight, norm_gains, norm_biases)
        expert_set = fetch_experts(expert_in, expert_out)
        ids_ext = padded(image_ids[batch_index] + 1, ((("dp", "expert"), 0),), rim_rows)
        route_plan = plan_routes(routes[batch_index], shard_experts)
        forward_state = run_forward(
            tokens[batch_index].astype(jnp.float32), ids_ext, route_plan, dense_set, expert_set
        )
        outputs.append(forward_state[-1].astype(jnp.bfloat16))
        saved_state.append((ids_ext, route_plan))
    gradients = (
        jnp.zeros((3, D, D), jnp.float32),
        jnp.zeros((D, D), jnp.float32),
        jnp.zeros((D, experts), jnp.float32),
        jnp.zeros((2, D), jnp.float32),
        jnp.zeros((2, D), jnp.float32),
        jnp.zeros((shard_experts, D, FF), jnp.float32),
        jnp.zeros((shard_experts, FF, D), jnp.float32),
    )
    input_grads = []
    for batch_index in range(MICRO):
        dense_set = fetch_dense(qkv_weight, out_weight, router_weight, norm_gains, norm_biases)
        expert_set = fetch_experts(expert_in, expert_out)
        ids_ext, route_plan = saved_state[batch_index]
        input_rows, gradients = run_backward(
            tokens[batch_index].astype(jnp.float32),
            ids_ext,
            route_plan,
            dense_set,
            expert_set,
            cotangent[batch_index].astype(jnp.float32),
            gradients,
        )
        input_grads.append(input_rows)
    grad_qkv, grad_out, grad_router, grad_gains, grad_biases, grad_in, grad_expert_out = gradients
    small = jnp.concatenate([grad_router, grad_gains.T, grad_biases.T], axis=1)
    small = jnp.pad(small, ((0, 0), (0, D - experts - 4)))
    packed = jnp.concatenate([grad_qkv, grad_out[None], small[None]], axis=0)
    packed = lax.psum_scatter(packed, ("dp", "expert"), scatter_dimension=1, tiled=True)
    dense_grads = (
        packed[:3],
        packed[3],
        packed[4][:, :experts],
        packed[4][:, experts : experts + 2].T,
        packed[4][:, experts + 2 : experts + 4].T,
    )
    expert_grads = (
        lax.psum_scatter(
            grad_in.astype(jnp.bfloat16), "dp", scatter_dimension=1, tiled=True
        ).astype(jnp.float32),
        lax.psum_scatter(
            grad_expert_out.astype(jnp.bfloat16), "dp", scatter_dimension=1, tiled=True
        ).astype(jnp.float32),
    )
    return (
        jnp.stack(outputs),
        jnp.stack(input_grads),
        dense_grads[0],
        dense_grads[1],
        dense_grads[2],
        dense_grads[3],
        dense_grads[4],
        expert_grads[0],
        expert_grads[1],
    )


MESH = pl.DeviceIdType.MESH
f32, bf16 = jnp.float32, jnp.bfloat16
VMEM_BYTES = 62 << 20


def mm(a, b):
    return jnp.dot(a, b, preferred_element_type=f32)


def mm_nt(a, b):
    return lax.dot_general(a, b, (((1,), (1,)), ((), ())), preferred_element_type=f32)


def normed(values, gain_row, bias_row):
    centre = jnp.mean(values, axis=-1, keepdims=True)
    offset = values - centre
    spread = jnp.mean(offset * offset, axis=-1, keepdims=True)
    return offset * lax.rsqrt(spread + norm_eps) * gain_row + bias_row


class Wire:
    def __init__(self, send_sems, recv_sems, other):
        self.send_sems, self.recv_sems, self.other = send_sems, recv_sems, other
        self.used, self.sent = 0, {}

    def roles(self, count=1):
        self.used += count
        return self.used - count

    def copy(self, send_role, recv_role, src, dst, device):
        return pltpu.make_async_remote_copy(
            src_ref=src,
            dst_ref=dst,
            send_sem=self.send_sems.at[send_role],
            recv_sem=self.recv_sems.at[recv_role],
            device_id=device,
            device_id_type=MESH,
        )

    def send(self, role, src, dst, device, recv_role=None):
        self.copy(role, role if recv_role is None else recv_role, src, dst, device).start()

    def arrive(self, role, like):
        self.copy(role, role, like, like, self.other).wait_recv()

    def left(self, role, like):
        self.copy(role, role, like, like, self.other).wait_send()


class Place:
    def __init__(self, nd, ne):
        self.nd, self.ne = nd, ne
        self.d, self.z = lax.axis_index("dp"), lax.axis_index("expert")
        d, z = self.d, self.z
        self.c = lax.rem(d, 2)
        self.sib_d = d + 1 - 2 * self.c
        self.sib = (self.sib_d, z)
        self.idx = d * ne + z
        last = (z == ne - 1).astype(jnp.int32)
        first = (z == 0).astype(jnp.int32)
        self.next = (lax.rem(d + last, nd), lax.rem(z + 1, ne))
        self.prev = (lax.rem(d + nd - first, nd), lax.rem(z + ne - 1, ne))
        self.up = (d, jnp.minimum(z + 1, ne - 1))
        self.down = (d, jnp.maximum(z - 1, 0))

    def chip(self, k):
        return lax.rem(self.d + 2 * k, self.nd)

    def enter(self):
        bar = pltpu.get_barrier_semaphore()

        def greet(device):
            pl.semaphore_signal(bar, inc=1, device_id=device, device_id_type=MESH)

        for k in range(1, self.nd):
            greet((lax.rem(self.d + k, self.nd), self.z))
        for k in range(1, self.ne):
            zk = lax.rem(self.z + k, self.ne)
            greet((self.d, zk))
            greet((self.sib_d, zk))
        greet(self.next)
        greet(self.prev)
        pl.semaphore_wait(bar, self.nd - 1 + 2 * (self.ne - 1) + 2)


class Chain:
    def __init__(self, wire, me, full):
        self.wire, self.me, self.full = wire, me, full
        n = me.ne
        self.up, self.dn = wire.roles(n - 1), wire.roles(n - 1)
        self.su, self.sd, self.so = wire.roles(n - 1), wire.roles(n - 1), wire.roles()

    def at(self, z):
        return self.full.at[z * 2 + self.me.c]

    def own(self, src):
        m, n = self.me, self.me.ne

        @pl.when(m.z < n - 1)
        def _():
            self.wire.send(self.up, src, self.at(m.z), m.up)

        @pl.when(m.z > 0)
        def _():
            self.wire.send(self.dn, src, self.at(m.z), m.down)

        self.wire.send(self.so, src, self.at(m.z), m.sib)

    def pump(self, k):
        m, n, w = self.me, self.me.ne, self.wire

        @pl.when(m.z >= k + 1)
        def _():
            block = self.at(m.z - 1 - k)
            w.arrive(self.up + k, block)
            if k + 1 < n - 1:

                @pl.when(m.z < n - 1)
                def _():
                    w.send(self.up + k + 1, block, block, m.up)

            w.send(self.su + k, block, block, m.sib)

        @pl.when(m.z + k + 1 < n)
        def _():
            block = self.at(m.z + 1 + k)
            w.arrive(self.dn + k, block)
            if k + 1 < n - 1:

                @pl.when(m.z > 0)
                def _():
                    w.send(self.dn + k + 1, block, block, m.down)

            w.send(self.sd + k, block, block, m.sib)

    def finish(self):
        m, n, w, like = self.me, self.me.ne, self.wire, self.full.at[0]
        w.arrive(self.so, like)
        for k in range(n - 1):

            @pl.when(m.z >= k + 1)
            def _():
                w.arrive(self.su + k, like)

            @pl.when(m.z + k + 1 < n)
            def _():
                w.arrive(self.sd + k, like)

    def drain(self):
        m, n, w, like = self.me, self.me.ne, self.wire, self.full.at[0]
        w.left(self.so, like)
        for k in range(n - 1):

            @pl.when((m.z < n - 1) & (m.z >= k))
            def _():
                w.left(self.up + k, like)

            @pl.when((m.z > 0) & (m.z + k < n))
            def _():
                w.left(self.dn + k, like)

            @pl.when(m.z >= k + 1)
            def _():
                w.left(self.su + k, like)

            @pl.when(m.z + k + 1 < n)
            def _():
                w.left(self.sd + k, like)


def front_kernel(
    nd,
    ne,
    tok,
    ids,
    routes,
    qkv,
    outw,
    small,
    win,
    wout,
    cot,
    o_block,
    o_din,
    o_dprobs,
    o_up,
    o_down,
    o_n2,
    o_probs,
    o_resid,
    o_mixed,
    o_qkv,
    o_lse,
    w_all,
    o_small,
    o_idr,
    s_src,
    s_all,
    hp,
    hn,
    ip,
    inx,
    gx,
    gd,
    wu,
    wd,
    rk_src,
    rk,
    hnorm,
    bias,
    d_wu,
    d_wd,
    pm,
    xs,
    ds,
    deo,
    xt,
    dt,
    gt,
    acc_eo,
    acc_di,
    ys,
    qo,
    cs,
    cr,
    ud,
    dgs,
    dg,
    send_sems,
    recv_sems,
    local_sems,
):
    me = Place(nd, ne)
    d, z, c = me.d, me.z, me.c
    rows = tok.shape[1]
    share = qkv.shape[1]
    experts = 2 * ne
    halo = hp.shape[1]
    ext = 3 * rows
    slots = 4 * rows // experts
    capacity = 5 * TOP * rows * nd * ne // (4 * experts)
    e = 2 * z + c
    wire = Wire(send_sems, recv_sems, me.sib)
    lane = lax.broadcasted_iota(jnp.int32, (1, 128), 1)

    before_row = (
        lax.broadcasted_iota(jnp.int32, (rows, rows), 0)
        > lax.broadcasted_iota(jnp.int32, (rows, rows), 1)
    ).astype(bf16)
    hots = []
    s_src[0:share, :] = small[...]
    s_src[share : share + 16, :] = jnp.zeros((16, 128), bf16)
    row16 = lax.broadcasted_iota(jnp.int32, (16, 128), 0)
    counts = jnp.zeros((16, 128), f32)
    for mb in range(MICRO):
        pair = [(routes[mb, :, k : k + 1] == lane).astype(f32) for k in range(TOP)]
        hots.append(pair)
        for k in range(TOP):
            counts = jnp.where(row16 == mb * TOP + k, jnp.sum(pair[k], axis=0, keepdims=True), counts)
    s_src[share : share + 16, :] = counts.astype(bf16)

    me.enter()

    r_dz = wire.roles(3 * (ne - 1))
    mine = pl.ds(pl.multiple_of(me.idx * share, 16), share)
    for k in range(1, ne):
        dev = (d, lax.rem(z + k, ne))
        wire.send(r_dz + 3 * (k - 1), qkv, w_all.at[pl.ds(0, 3), mine], dev)
        wire.send(r_dz + 3 * (k - 1) + 1, outw, w_all.at[3, mine], dev)
        wire.send(r_dz + 3 * (k - 1) + 2, s_src, s_all.at[me.idx], dev)
    local = [
        pltpu.make_async_copy(qkv, w_all.at[pl.ds(0, 3), mine], local_sems.at[0]),
        pltpu.make_async_copy(outw, w_all.at[3, mine], local_sems.at[1]),
        pltpu.make_async_copy(s_src, s_all.at[me.idx], local_sems.at[2]),
    ]
    for cp in local:
        cp.start()
    r_id = wire.roles(2)
    wire.send(r_id, ids, ip, me.next)
    wire.send(r_id + 1, ids, inx, me.prev)
    r_h = wire.roles(2 * MICRO)
    for mb in range(MICRO):
        wire.send(r_h + 2 * mb, tok.at[mb, pl.ds(rows - halo, halo)], hp.at[mb], me.next)
        wire.send(r_h + 2 * mb + 1, tok.at[mb, pl.ds(0, halo)], hn.at[mb], me.prev)
    g_d = [Chain(wire, me, gd.at[mb]) for mb in range(MICRO)]
    g_x = [Chain(wire, me, gx.at[mb]) for mb in range(MICRO)]
    own_d = [
        pltpu.make_async_copy(cot.at[mb], gd.at[mb, z * 2 + c], local_sems.at[3 + mb])
        for mb in range(MICRO)
    ]
    for cp in own_d:
        cp.start()
    g_d[0].own(cot.at[0])

    for cp in local:
        cp.wait()
    for k in range(1, ne):
        wire.arrive(r_dz + 3 * (k - 1), qkv)
        wire.arrive(r_dz + 3 * (k - 1) + 1, outw)
        wire.arrive(r_dz + 3 * (k - 1) + 2, s_src)

    def column(dd):
        at = pl.ds(pl.multiple_of(dd * (ne * share), 16), ne * share)
        return w_all.at[:, at], s_all.at[pl.ds(dd * ne, ne)]

    chips = nd // 2
    r_dx = wire.roles(2 * (chips - 1))
    r_ds = wire.roles(2 * chips)
    blk, sblk = column(d)
    for k in range(1, chips):
        wire.send(r_dx + 2 * (k - 1), blk, blk, (me.chip(k), z))
        wire.send(r_dx + 2 * (k - 1) + 1, sblk, sblk, (me.chip(k), z))
    wire.send(r_ds, blk, blk, me.sib)
    wire.send(r_ds + 1, sblk, sblk, me.sib)
    up_rows, down_rows = win.shape[1], wout.shape[1]
    at_up = pl.ds(pl.multiple_of(d * up_rows, 16), up_rows)
    at_down = pl.ds(pl.multiple_of(d * down_rows, 16), down_rows)
    r_w = wire.roles(2 * (nd - 1))
    own_w = [
        pltpu.make_async_copy(win.at[c], wu.at[at_up], local_sems.at[5]),
        pltpu.make_async_copy(wout.at[c], wd.at[at_down], local_sems.at[6]),
    ]
    for cp in own_w:
        cp.start()
    for k in range(1, nd):
        dd = lax.rem(d + k, nd)
        cc = lax.rem(dd, 2)
        wire.send(r_w + 2 * (k - 1), win.at[cc], wu.at[at_up], (dd, z))
        wire.send(r_w + 2 * (k - 1) + 1, wout.at[cc], wd.at[at_down], (dd, z))
    g_d[0].pump(0)
    for k in range(1, chips):
        wire.arrive(r_dx + 2 * (k - 1), blk)
        wire.arrive(r_dx + 2 * (k - 1) + 1, sblk)
        b, sb = column(lax.rem(d + nd - 2 * k, nd))
        wire.send(r_ds + 2 * k, b, b, me.sib)
        wire.send(r_ds + 2 * k + 1, sb, sb, me.sib)
    for k in range(chips):
        wire.arrive(r_ds + 2 * k, blk)
        wire.arrive(r_ds + 2 * k + 1, sblk)

    o_small[...] = s_all[:, 0:share, :].reshape(D, 128).astype(f32)
    s_rows = o_small[...].T
    all_counts = s_all[:, share : share + 16, :].astype(f32)
    ahead = lax.broadcasted_iota(jnp.int32, all_counts.shape, 0) < me.idx
    before = jnp.sum(jnp.where(ahead, all_counts, 0.0), axis=0)
    total = jnp.sum(all_counts, axis=0)
    gains = [s_rows[experts + k : experts + k + 1, :] for k in range(2)]
    biases = [s_rows[experts + 2 + k : experts + 3 + k, :] for k in range(2)]

    for mb in range(MICRO):
        one, two = hots[mb]
        rank_one = mm(before_row, one.astype(bf16))
        rank_two = mm(before_row, two.astype(bf16))
        b1, b2 = before[2 * mb : 2 * mb + 1], before[2 * mb + 1 : 2 * mb + 2]
        t1 = total[2 * mb : 2 * mb + 1]
        place_one = jnp.sum(one * (b1 + rank_one), axis=1, keepdims=True)
        place_two = jnp.sum(two * (t1 + b2 + rank_two), axis=1, keepdims=True)
        kept = one * (place_one < capacity).astype(f32) + two * (place_two < capacity).astype(f32)
        ranks = jnp.where(kept > 0.0, rank_one + rank_two, -1.0)
        rk_src[mb] = ranks.T[0:experts, :]
    r_rk = wire.roles(2 * ne)
    s_me = z * 2 + c
    for k in range(ne):
        zk = lax.rem(z + k, ne)
        if k > 0:
            wire.send(r_rk + 2 * k, rk_src, rk.at[s_me], (d, zk))
        wire.send(r_rk + 2 * k + 1, rk_src, rk.at[s_me], (me.sib_d, zk))
    rk[s_me] = rk_src[...]
    g_d[0].pump(1)

    wire.arrive(r_id, ids)
    wire.arrive(r_id + 1, ids)
    pos = lax.broadcasted_iota(jnp.int32, (1, rows), 1)
    gap = rows - halo
    for mb in range(MICRO):
        here = ids[mb : mb + 1, :].astype(f32)
        below = jnp.where((pos >= gap) & (me.idx > 0), ip[mb : mb + 1, :].astype(f32), -1.0)
        above = jnp.where(
            (pos < halo) & (me.idx < nd * ne - 1), inx[mb : mb + 1, :].astype(f32), -1.0
        )
        o_idr[mb] = jnp.concatenate([below, here, above], axis=1)

    zero_gap = jnp.zeros((gap, D), bf16)
    hnorm[0:gap, :] = zero_gap
    hnorm[ext - gap : ext, :] = zero_gap
    scale = 1.0 / math.sqrt(HEAD_DIM)
    for mb in range(MICRO):
        wire.arrive(r_h + 2 * mb, hp.at[mb])
        wire.arrive(r_h + 2 * mb + 1, hn.at[mb])

        def put(value, start):
            hnorm[start : start + value.shape[0], :] = normed(
                value.astype(f32), gains[0], biases[0]
            ).astype(bf16)

        put(hp[mb], gap)
        put(tok[mb], rows)
        put(hn[mb], 2 * rows)
        for k in range(3):
            for r in range(3):
                part = slice(r * rows, (r + 1) * rows)
                o_qkv[mb, k, part, :] = mm(hnorm[part, :], w_all[k]).astype(bf16)
        g_d[0].pump(2) if mb == 0 else g_x[0].pump(0)
        idr = o_idr[mb]
        idc = jnp.broadcast_to(idr[:, rows : 2 * rows], (128, rows)).T[:, 0:1]
        bias[...] = jnp.where(idc == idr, 0.0, neg_big)
        o_lse[mb] = jnp.zeros((rows, 128), f32)

        @pl.loop(0, HEADS // 2)
        def _(pair):
            at = pl.ds(pl.multiple_of(pair * 128, 128), 128)
            query = o_qkv[mb, 0, rows : 2 * rows, at]
            key = o_qkv[mb, 1, :, at]
            value = o_qkv[mb, 2, :, at]
            mixed = jnp.zeros((rows, 128), f32)
            lse = o_lse[mb]
            for half in range(2):
                keep = (lane < 64) if half == 0 else (lane >= 64)
                q = jnp.where(keep, query, jnp.zeros_like(query))
                v = jnp.where(keep, value, jnp.zeros_like(value))
                s = mm_nt(q, key) * scale + bias[...]
                top = jnp.max(s, axis=-1, keepdims=True)
                p = jnp.exp(s - top)
                total_p = jnp.sum(p, axis=-1, keepdims=True)
                mixed = mixed + mm((p * (1.0 / total_p)).astype(bf16), v)
                lse = jnp.where(lane == 2 * pair + half, top + jnp.log(total_p), lse)
            o_lse[mb] = lse
            o_mixed[mb, :, at] = mixed.astype(bf16)

        if mb == 1:
            g_x[0].pump(1)
        resid = tok[mb].astype(f32) + mm(o_mixed[mb], w_all[3])
        o_resid[mb] = resid
        n2 = normed(resid, gains[1], biases[1]).astype(bf16)
        o_n2[mb] = n2
        gx[mb, s_me] = n2
        g_x[mb].own(gx.at[mb, s_me])
        if mb == 0:
            g_d[1].own(cot.at[1])
        logits = mm(n2, o_small[...].astype(bf16))
        logits = jnp.where(lane < experts, logits, neg_big)
        p = jnp.exp(logits - jnp.max(logits, axis=-1, keepdims=True))
        o_probs[mb] = p / jnp.sum(p, axis=-1, keepdims=True)
    g_x[0].pump(2)

    for cp in own_w + own_d:
        cp.wait()
    for k in range(1, nd):
        wire.arrive(r_w + 2 * (k - 1), win.at[0])
        wire.arrive(r_w + 2 * (k - 1) + 1, wout.at[0])
    for k in range(ne):
        if k > 0:
            wire.arrive(r_rk + 2 * k, rk_src)
        wire.arrive(r_rk + 2 * k + 1, rk_src)
    g_d[0].finish()
    g_x[0].finish()
    d_wu[...] = jnp.zeros_like(d_wu)
    d_wd[...] = jnp.zeros_like(d_wd)

    r_cx = wire.roles(2 * MICRO * ne)
    r_up = wire.roles(2 * MICRO * ne)
    r_dn = wire.roles(2 * MICRO * ne)
    r_dg = wire.roles(MICRO * 2 * ne)
    sub = lax.broadcasted_iota(jnp.int32, (slots, rows), 0).astype(f32)
    tile = 2 * slots
    chunk = 512

    def start_sums(mb):
        for t in range(2):
            for zp in range(ne):
                wire.arrive(r_cx + (mb * 2 + t) * ne + zp, qo.at[0, 0, 0])
                qo[mb, t, zp] = (qo[mb, t, zp].astype(f32) + cr[mb, t, zp].astype(f32)).astype(bf16)

        @pl.when(z == 0)
        def _():
            for t in range(2):
                for to in range(ne - 1, 0, -1):
                    wire.send(
                        r_up + (mb * 2 + t) * ne + to, qo.at[mb, t, to], ud.at[mb, t, to], me.up
                    )

        @pl.when(z == ne - 1)
        def _():
            for t in range(2):
                for to in range(ne - 1):
                    slot = jnp.where(z - 1 == to, ne, to)
                    wire.send(
                        r_dn + (mb * 2 + t) * ne + to, qo.at[mb, t, to], ud.at[mb, t, slot], me.down
                    )

    def pass_sums(mb):
        for t in range(2):
            for k in range(ne - 1):
                to = ne - 1 - k

                @pl.when((z > 0) & (z < to))
                def _():
                    wire.arrive(r_up + (mb * 2 + t) * ne + to, qo.at[0, 0, 0])
                    qo[mb, t, to] = (
                        qo[mb, t, to].astype(f32) + ud[mb, t, to].astype(f32)
                    ).astype(bf16)
                    wire.send(
                        r_up + (mb * 2 + t) * ne + to, qo.at[mb, t, to], ud.at[mb, t, to], me.up
                    )

                @pl.when((z < ne - 1) & (z > k))
                def _():
                    wire.arrive(r_dn + (mb * 2 + t) * ne + k, qo.at[0, 0, 0])
                    qo[mb, t, k] = (
                        qo[mb, t, k].astype(f32) + ud[mb, t, k].astype(f32)
                    ).astype(bf16)
                    slot = jnp.where(z - 1 == k, ne, k)
                    wire.send(
                        r_dn + (mb * 2 + t) * ne + k, qo.at[mb, t, k], ud.at[mb, t, slot], me.down
                    )

    def end_sums(mb, t):
        out = qo[mb, t, z].astype(f32)
        acc_eo[...] = out

        @pl.when(z > 0)
        def _():
            wire.arrive(r_up + (mb * 2 + t) * ne + z, qo.at[0, 0, 0])
            acc_eo[...] += ud[mb, t, z].astype(f32)

        @pl.when(z < ne - 1)
        def _():
            wire.arrive(r_dn + (mb * 2 + t) * ne + z, qo.at[0, 0, 0])
            acc_eo[...] += ud[mb, t, ne].astype(f32)

        return acc_eo[...]

    @pl.loop(0, MICRO * ne)
    def _(i):
        mb, zi = i // ne, lax.rem(i, ne)
        zp = lax.rem(zi * (ne - 1), ne)

        @pl.when(i == ne)
        def _():
            start_sums(0)
            for k in range(ne - 1):
                g_d[1].pump(k)
                g_x[1].pump(k)
            g_d[1].finish()
            g_x[1].finish()

        for cc in range(2):
            s = zp * 2 + cc
            at = slice(cc * slots, (cc + 1) * slots)
            pick = (sub == rk[s, mb, pl.ds(e, 1), :]).astype(bf16)
            pm[cc] = pick
            xs[at, :] = mm(pick, gx[mb, s]).astype(bf16)
            ds[at, :] = mm(pick, gd[mb, s]).astype(bf16)
        x = xs[...]
        logits = mm(x, o_small[...].astype(bf16))
        logits = jnp.where(lane < experts, logits, neg_big)
        p = jnp.exp(logits - jnp.max(logits, axis=-1, keepdims=True))
        p = p / jnp.sum(p, axis=-1, keepdims=True)
        gate = jnp.sum(jnp.where(lane == e, p, 0.0), axis=-1, keepdims=True)
        gt[...] = jnp.broadcast_to(gate, (tile, 128))
        dy = (gate * ds[...].astype(f32)).astype(bf16)
        deo[...] = dy
        xt[...] = x.T
        dt[...] = dy.T
        acc_eo[...] = jnp.zeros_like(acc_eo)
        acc_di[...] = jnp.zeros_like(acc_di)

        @pl.loop(0, FF // chunk)
        def _(f):
            at = pl.ds(pl.multiple_of(f * chunk, chunk), chunk)
            pre = mm(xs[...], wu[:, at])
            sq = pre * pre
            k0 = math.sqrt(2.0 / math.pi)
            th = jnp.tanh(pre * (k0 + (k0 * 0.044715) * sq))
            half = 0.5 + 0.5 * th
            act = (pre * half).astype(bf16)
            slope = half + (0.5 * pre) * (1.0 - th * th) * (k0 + (3.0 * k0 * 0.044715) * sq)
            acc_eo[...] += mm(act, wd[at, :])
            d_act = mm_nt(deo[...], wd[at, :])
            d_pre = (slope * d_act).astype(bf16)
            acc_di[...] += mm_nt(d_pre, wu[:, at])
            d_wu[:, at] += mm(xt[...], d_pre)
            d_wd[:, at] += mm(dt[...], act)

        eo = acc_eo[...].astype(bf16).astype(f32)
        d_gate = jnp.sum(ds[...].astype(f32) * eo, axis=-1, keepdims=True)
        ys[0] = acc_di[...].astype(bf16)
        ys[1] = (gt[:, 0:1] * eo).astype(bf16)
        for own in range(2):
            cc = c if own else 1 - c
            back = pm[cc].T
            at = pl.ds(pl.multiple_of(cc * slots, slots), slots)
            for t in range(2):
                moved = mm(back, ys[t, at, :]).astype(bf16)
                if own:
                    qo[mb, t, zp] = moved
                else:
                    cs[mb, t, zp] = moved
        for t in range(2):
            role = r_cx + (mb * 2 + t) * ne + zp
            wire.send(role, cs.at[mb, t, zp], cr.at[mb, t, zp], me.sib)
        for cc in range(2):
            at = slice(cc * slots, (cc + 1) * slots)
            line = jnp.sum(pm[cc].astype(f32) * d_gate[at], axis=0, keepdims=True)
            to = zp * 2 + cc
            dgs[mb, to] = jnp.broadcast_to(line, (8, rows))

            @pl.when(to != s_me)
            def _():
                wire.send(
                    r_dg + mb * 2 * ne + to,
                    dgs.at[mb, to],
                    dg.at[mb, e],
                    (d - c + cc, zp),
                    recv_role=r_dg + mb * 2 * ne + s_me,
                )

            @pl.when(to == s_me)
            def _():
                dg[mb, e] = jnp.broadcast_to(line, (8, rows))

    pass_sums(0)
    start_sums(1)
    g_d[0].drain()
    out_copies = []
    for h in range(2):
        for q in range(4):
            at = (slice(h * 256, (h + 1) * 256), slice(q * chunk, (q + 1) * chunk))
            wu[at] = d_wu[at].astype(bf16)
            gd[0, h * 4 + q] = d_wd[at].astype(bf16)
            to = o_down.at[pl.ds(h * 256, 256), pl.ds(q * chunk, chunk)]
            out_copies.append(pltpu.make_async_copy(gd.at[0, h * 4 + q], to, local_sems.at[h * 4 + q]))
    out_copies.append(pltpu.make_async_copy(wu, o_up, local_sems.at[8]))
    for cp in out_copies:
        cp.start()

    def outputs(mb):
        o_din[mb] = end_sums(mb, 0)
        o_block[mb] = (o_resid[mb] + end_sums(mb, 1)).astype(bf16)

    outputs(0)
    pass_sums(1)
    outputs(1)
    for mb in range(MICRO):
        for s in range(2 * ne):

            @pl.when(s != s_me)
            def _():
                wire.arrive(r_dg + mb * 2 * ne + s, dgs.at[0, 0])

        groups = []
        sub8 = lax.broadcasted_iota(jnp.int32, (8, rows), 0)
        for base in range(0, experts, 8):
            group = dg[mb, base]
            for j in range(1, 8):
                group = jnp.where(sub8 == j, dg[mb, base + j], group)
            groups.append(group)
        lines = jnp.concatenate(groups + [jnp.zeros((128 - experts, rows), f32)], axis=0)
        o_dprobs[mb] = lines.T

    for cp in out_copies:
        cp.wait()
    for k in range(1, ne):
        wire.left(r_dz + 3 * (k - 1), qkv)
        wire.left(r_dz + 3 * (k - 1) + 1, outw)
        wire.left(r_dz + 3 * (k - 1) + 2, s_src)
    wire.left(r_id, ids)
    wire.left(r_id + 1, ids)
    for k in range(2 * MICRO):
        wire.left(r_h + k, hp.at[0])
    for k in range(1, chips):
        wire.left(r_dx + 2 * (k - 1), blk)
        wire.left(r_dx + 2 * (k - 1) + 1, sblk)
    for k in range(chips):
        wire.left(r_ds + 2 * k, blk)
        wire.left(r_ds + 2 * k + 1, sblk)
    for k in range(1, nd):
        wire.left(r_w + 2 * (k - 1), win.at[0])
        wire.left(r_w + 2 * (k - 1) + 1, wout.at[0])
    for k in range(ne):
        if k > 0:
            wire.left(r_rk + 2 * k, rk_src)
        wire.left(r_rk + 2 * k + 1, rk_src)
    for g in [g_d[1]] + g_x:
        g.drain()
    for mb in range(MICRO):
        for t in range(2):
            base = (mb * 2 + t) * ne
            for zp in range(ne):
                wire.left(r_cx + base + zp, qo.at[0, 0, 0])
            for to in range(1, ne):

                @pl.when(z < to)
                def _():
                    wire.left(r_up + base + to, qo.at[0, 0, 0])

            for to in range(ne - 1):

                @pl.when(z > to)
                def _():
                    wire.left(r_dn + base + to, qo.at[0, 0, 0])

        for s in range(2 * ne):

            @pl.when(s != s_me)
            def _():
                wire.left(r_dg + mb * 2 * ne + s, dgs.at[0, 0])

    assert wire.used <= ROLES


ROLES = 240


def front(nd, ne, tokens, image_ids, routes, qkv, outw, small, win, wout, cot):
    rows, share = tokens.shape[1], qkv.shape[1]
    halo = -(-(IMG - 1) // 16) * 16
    experts = 2 * ne
    slots = 4 * rows // experts
    shape = jax.ShapeDtypeStruct
    outs = (
        shape((MICRO, rows, D), bf16),
        shape((MICRO, rows, D), f32),
        shape((MICRO, rows, 128), f32),
        shape((D, FF), bf16),
        shape((D, FF), bf16),
        shape((MICRO, rows, D), bf16),
        shape((MICRO, rows, 128), f32),
        shape((MICRO, rows, D), f32),
        shape((MICRO, rows, D), bf16),
        shape((MICRO, 3, 3 * rows, D), bf16),
        shape((MICRO, rows, 128), f32),
        shape((4, D, D), bf16),
        shape((D, 128), f32),
        shape((MICRO, 1, 3 * rows), f32),
    )
    vmem, anywhere = pl.BlockSpec(memory_space=pltpu.VMEM), pl.BlockSpec(memory_space=pl.ANY)
    v = pltpu.VMEM
    return pl.pallas_call(
        functools.partial(front_kernel, nd, ne),
        out_shape=outs,
        in_specs=[vmem, vmem, vmem, anywhere, anywhere, vmem, anywhere, anywhere, anywhere],
        out_specs=[anywhere if k in (3, 4) else vmem for k in range(len(outs))],
        scratch_shapes=[
            v((share + 16, 128), bf16),
            v((nd * ne, share + 16, 128), bf16),
            v((MICRO, halo, D), bf16),
            v((MICRO, halo, D), bf16),
            v((MICRO, rows), jnp.int32),
            v((MICRO, rows), jnp.int32),
            v((MICRO, 2 * ne, rows, D), bf16),
            v((MICRO, 2 * ne, rows, D), bf16),
            v((D, FF), bf16),
            v((FF, D), bf16),
            v((MICRO, experts, rows), f32),
            v((2 * ne, MICRO, experts, rows), f32),
            v((3 * rows, D), bf16),
            v((rows, 3 * rows), f32),
            v((D, FF), f32),
            v((D, FF), f32),
            v((2, slots, rows), bf16),
            v((2 * slots, D), bf16),
            v((2 * slots, D), bf16),
            v((2 * slots, D), bf16),
            v((D, 2 * slots), bf16),
            v((D, 2 * slots), bf16),
            v((2 * slots, 128), f32),
            v((2 * slots, D), f32),
            v((2 * slots, D), f32),
            v((2, 2 * slots, D), bf16),
            v((MICRO, 2, ne, rows, D), bf16),
            v((MICRO, 2, ne, rows, D), bf16),
            v((MICRO, 2, ne, rows, D), bf16),
            v((MICRO, 2, ne + 1, rows, D), bf16),
            v((MICRO, 2 * ne, 8, rows), f32),
            v((MICRO, experts, 8, rows), f32),
            pltpu.SemaphoreType.DMA((ROLES,)),
            pltpu.SemaphoreType.DMA((ROLES,)),
            pltpu.SemaphoreType.DMA((9,)),
        ],
        compiler_params=pltpu.CompilerParams(
            collective_id=0, has_side_effects=True, vmem_limit_bytes=VMEM_BYTES
        ),
        name="front",
    )(tokens, image_ids, routes, qkv, outw, small, win, wout, cot)


def mm_exact(a, b):
    return jnp.dot(a, b, preferred_element_type=f32, precision=highest)


def back_kernel(
    nd,
    ne,
    tok,
    cot,
    d_in,
    d_probs,
    up,
    down,
    n2,
    probs,
    resid,
    mixed,
    qkv,
    lse,
    w,
    small,
    idr,
    o_input,
    o_dense,
    o_small,
    o_up,
    o_down,
    gu,
    gd,
    d_res,
    dm,
    stat_src,
    stat_p,
    stat_n,
    hp,
    hn,
    stats,
    bias,
    dp,
    gw,
    gs,
    gwb,
    gsb,
    rc,
    rcs,
    sx,
    sxs,
    rx,
    rxs,
    sz,
    szs,
    rz,
    rzs,
    send_sems,
    recv_sems,
    local_sems,
):
    me = Place(nd, ne)
    d, z, c = me.d, me.z, me.c
    rows = tok.shape[1]
    experts = 2 * ne
    halo = hp.shape[1]
    gap = rows - halo
    chips = nd // 2
    wire = Wire(send_sems, recv_sems, me.sib)
    lane = lax.broadcasted_iota(jnp.int32, (1, 128), 1)
    up_rows, down_rows = gu.shape[1], gd.shape[2]
    part = D // nd
    share = part // ne
    me.enter()

    r_g = wire.roles(2 * (nd - 1))

    def up_of(dd):
        return up.at[pl.ds(pl.multiple_of(dd * up_rows, 16), up_rows)]

    def down_of(dd):
        return down.at[:, pl.ds(pl.multiple_of(dd * down_rows, 128), down_rows)]

    own_g = [
        pltpu.make_async_copy(up_of(d), gu.at[d], local_sems.at[0]),
        pltpu.make_async_copy(down_of(d), gd.at[d], local_sems.at[1]),
    ]
    for cp in own_g:
        cp.start()
    for k in range(1, nd):
        dd = lax.rem(d + k, nd)
        wire.send(r_g + 2 * (k - 1), up_of(dd), gu.at[d], (dd, z))
        wire.send(r_g + 2 * (k - 1) + 1, down_of(dd), gd.at[d], (dd, z))

    s_rows = small[...].T
    gains = [s_rows[experts + k : experts + k + 1, :] for k in range(2)]
    router = jnp.where(lane < experts, small[...], 0.0)
    head_of = (
        lax.broadcasted_iota(jnp.int32, (D, 128), 0) // HEAD_DIM
        == lax.broadcasted_iota(jnp.int32, (D, 128), 1)
    ).astype(f32)

    def norm_back(values, dn, gain):
        offset = values - jnp.mean(values, axis=-1, keepdims=True)
        inv = lax.rsqrt(jnp.mean(offset * offset, axis=-1, keepdims=True) + norm_eps)
        hat = offset * inv
        q = dn * gain
        dv = inv * (
            q
            - jnp.mean(q, axis=-1, keepdims=True)
            - hat * jnp.mean(q * hat, axis=-1, keepdims=True)
        )
        return dv, jnp.sum(dn * hat, axis=0, keepdims=True), jnp.sum(dn, axis=0, keepdims=True)

    r_h = wire.roles(4 * MICRO)
    norm_sums = [jnp.zeros((1, D), f32) for _ in range(4)]
    zero_gap = jnp.zeros((gap, D), bf16)
    own = slice(rows, 2 * rows)
    for mb in range(MICRO):
        prob, dpr = probs[mb], d_probs[mb]
        d_logits = prob * (dpr - jnp.sum(prob * dpr, axis=-1, keepdims=True))
        dn2 = d_in[mb] + lax.dot_general(
            d_logits,
            router,
            (((1,), (1,)), ((), ())),
            preferred_element_type=f32,
            precision=highest,
        )
        dv, d_gain, d_bias = norm_back(resid[mb], dn2, gains[1])
        norm_sums[1] += d_gain
        norm_sums[3] += d_bias
        d_resid = cot[mb].astype(f32) + dv
        d_res[mb] = d_resid
        d_attn = d_resid.astype(bf16)
        d_mixed = mm_nt(d_attn, w[3]).astype(bf16)
        dm[mb, own, :] = d_mixed
        delta = mm_exact(d_mixed.astype(f32) * mixed[mb].astype(f32), head_of)
        stat_src[mb, 0] = lse[mb].T[0:HEADS, :]
        stat_src[mb, 1] = delta.T[0:HEADS, :]
        low, high = pl.ds(rows, halo), pl.ds(2 * rows - halo, halo)
        wire.send(r_h + 4 * mb, dm.at[mb, high], hp.at[mb], me.next)
        wire.send(r_h + 4 * mb + 1, stat_src.at[mb], stat_p.at[mb], me.next)
        wire.send(r_h + 4 * mb + 2, dm.at[mb, low], hn.at[mb], me.prev)
        wire.send(r_h + 4 * mb + 3, stat_src.at[mb], stat_n.at[mb], me.prev)
        g_out = mm(mixed[mb].T, d_attn)
        g_router = mm_exact(n2[mb].astype(f32).T, d_logits)
        if mb == 0:
            gw[3] = g_out
            gs[...] = g_router
        else:
            gw[3] += g_out
            gs[...] += g_router

    scale = 1.0 / math.sqrt(HEAD_DIM)
    for mb in range(MICRO):
        ids = idr[mb]
        idc = jnp.broadcast_to(ids[:, own], (128, rows)).T[:, 0:1]
        bias[...] = jnp.where(idc == ids, 0.0, neg_big)
        dst = jnp.zeros((rows, 128), f32)
        delta_cols = jnp.concatenate(
            [stat_src[mb, 1], jnp.zeros((128 - HEADS, rows), f32)], axis=0
        ).T

        @pl.loop(0, HEADS // 2)
        def _(pair):
            at = pl.ds(pl.multiple_of(pair * 128, 128), 128)
            query, grad = qkv[mb, 0, own, at], dm[mb, own, at]
            key, value = qkv[mb, 1, :, at], qkv[mb, 2, :, at]
            dq = jnp.zeros((rows, 128), f32)
            for half in range(2):
                keep = (lane < 64) if half == 0 else (lane >= 64)
                h = 2 * pair + half
                q = jnp.where(keep, query, jnp.zeros_like(query))
                g = jnp.where(keep, grad, jnp.zeros_like(grad))
                k = jnp.where(keep, key, jnp.zeros_like(key))
                lse_col = jnp.sum(jnp.where(lane == h, lse[mb], 0.0), axis=1, keepdims=True)
                delta_col = jnp.sum(jnp.where(lane == h, delta_cols, 0.0), axis=1, keepdims=True)
                p = jnp.exp(mm_nt(q, key) * scale + bias[...] - lse_col)
                ds = (p * (mm_nt(g, value) - delta_col)).astype(bf16)
                dq = dq + mm(ds, k)
            dp[0, :, at] = (dq * scale).astype(bf16)

        wire.arrive(r_h + 4 * mb, hp.at[mb])
        wire.arrive(r_h + 4 * mb + 1, stat_src.at[mb])
        wire.arrive(r_h + 4 * mb + 2, hp.at[mb])
        wire.arrive(r_h + 4 * mb + 3, stat_src.at[mb])
        dm[mb, 0:gap, :] = zero_gap
        dm[mb, gap:rows, :] = hp[mb]
        dm[mb, 2 * rows : 2 * rows + halo, :] = hn[mb]
        dm[mb, 2 * rows + halo : 3 * rows, :] = zero_gap
        for k in range(2):
            stats[k, :, 0:rows] = stat_p[mb, k]
            stats[k, :, own] = stat_src[mb, k]
            stats[k, :, 2 * rows : 3 * rows] = stat_n[mb, k]

        @pl.loop(0, HEADS // 2)
        def _(pair):
            at = pl.ds(pl.multiple_of(pair * 128, 128), 128)
            query, grad = qkv[mb, 0, :, at], dm[mb, :, at]
            key, value = qkv[mb, 1, own, at], qkv[mb, 2, own, at]
            dk = jnp.zeros((rows, 128), f32)
            dv = jnp.zeros((rows, 128), f32)
            for half in range(2):
                keep = (lane < 64) if half == 0 else (lane >= 64)
                h = 2 * pair + half
                q = jnp.where(keep, query, jnp.zeros_like(query))
                g = jnp.where(keep, grad, jnp.zeros_like(grad))
                k = jnp.where(keep, key, jnp.zeros_like(key))
                v = jnp.where(keep, value, jnp.zeros_like(value))
                p = jnp.exp(mm_nt(k, query) * scale + bias[...] - stats[0, pl.ds(h, 1), :])
                ds = (p * (mm_nt(v, grad) - stats[1, pl.ds(h, 1), :])).astype(bf16)
                dk = dk + mm(ds, q)
                dv = dv + mm(p.astype(bf16), g)
            dp[1, :, at] = (dk * scale).astype(bf16)
            dp[2, :, at] = dv.astype(bf16)

        token = tok[mb].astype(f32)
        n1t = normed(token, gains[0], s_rows[experts + 2 : experts + 3, :]).astype(bf16).T
        dn1 = jnp.zeros((rows, D), f32)
        for k in range(3):
            dn1 = dn1 + mm_nt(dp[k], w[k])
            g_part = mm(n1t, dp[k])
            if mb == 0:
                gw[k] = g_part
            else:
                gw[k] += g_part
        dv, d_gain, d_bias = norm_back(token, dn1, gains[0])
        norm_sums[0] += d_gain
        norm_sums[2] += d_bias
        o_input[mb] = (d_res[mb] + dv).astype(bf16)

    rows128 = lax.broadcasted_iota(jnp.int32, (128, D), 0)
    norm_rows = jnp.zeros((128, D), f32)
    for k in range(4):
        norm_rows = jnp.where(rows128 == experts + k, norm_sums[k], norm_rows)
    gs[...] = jnp.where(lane < experts, gs[...], norm_rows.T)

    def of(dd):
        return pl.ds(pl.multiple_of(dd * part, 16), part)

    r_c = wire.roles(2 * chips)
    r_x = wire.roles(2 * (chips - 1))
    r_z = wire.roles(2 * (ne - 1))
    for k in range(chips):
        dd = 2 * k + 1 - c
        for m in range(4):
            gwb[k, m] = gw[m, of(dd), :].astype(bf16)
        gsb[k] = gs[of(dd), :]
        wire.send(r_c + 2 * k, gwb.at[k], rc.at[k], me.sib)
        wire.send(r_c + 2 * k + 1, gsb.at[k], rcs.at[k], me.sib)
    for k in range(chips):
        wire.arrive(r_c + 2 * k, rc.at[k])
        wire.arrive(r_c + 2 * k + 1, rcs.at[k])
    my_chip = d // 2
    for k in range(1, chips):
        to = lax.rem(my_chip + k, chips)
        dd = 2 * to + c
        for m in range(4):
            sx[k, m] = (gw[m, of(dd), :] + rc[to, m].astype(f32)).astype(bf16)
        sxs[k] = gs[of(dd), :] + rcs[to]
        wire.send(r_x + 2 * (k - 1), sx.at[k], rx.at[k], (dd, z))
        wire.send(r_x + 2 * (k - 1) + 1, sxs.at[k], rxs.at[k], (dd, z))
    total = [gw[m, of(d), :] + rc[my_chip, m].astype(f32) for m in range(4)]
    total_s = gs[of(d), :] + rcs[my_chip]
    for k in range(1, chips):
        wire.arrive(r_x + 2 * (k - 1), rx.at[k])
        wire.arrive(r_x + 2 * (k - 1) + 1, rxs.at[k])
        total = [total[m] + rx[k, m].astype(f32) for m in range(4)]
        total_s = total_s + rxs[k]
    for m in range(4):
        gw[m, 0:part, :] = total[m]
    gs[0:part, :] = total_s
    for k in range(1, ne):
        to = lax.rem(z + k, ne)
        at = pl.ds(pl.multiple_of(to * share, 16), share)
        for m in range(4):
            sz[k, m] = gw[m, at, :].astype(bf16)
        szs[k] = gs[at, :]
        wire.send(r_z + 2 * (k - 1), sz.at[k], rz.at[k], (d, to))
        wire.send(r_z + 2 * (k - 1) + 1, szs.at[k], rzs.at[k], (d, to))

    for cp in own_g:
        cp.wait()
    for k in range(1, nd):
        wire.arrive(r_g + 2 * (k - 1), gu.at[0])
        wire.arrive(r_g + 2 * (k - 1) + 1, gd.at[0])
    for x in range(2):
        o_up[x] = sum(gu[2 * k + x].astype(f32) for k in range(chips))
        o_down[x] = sum(gd[2 * k + x].astype(f32) for k in range(chips)).T

    at = pl.ds(pl.multiple_of(z * share, 16), share)
    for k in range(1, ne):
        wire.arrive(r_z + 2 * (k - 1), rz.at[k])
        wire.arrive(r_z + 2 * (k - 1) + 1, rzs.at[k])
    for m in range(4):
        o_dense[m] = gw[m, at, :] + sum(rz[k, m].astype(f32) for k in range(1, ne))
    o_small[...] = gs[at, :] + sum(rzs[k] for k in range(1, ne))

    for k in range(1, nd):
        wire.left(r_g + 2 * (k - 1), gu.at[0])
        wire.left(r_g + 2 * (k - 1) + 1, gd.at[0])
    for mb in range(MICRO):
        for k in range(2):
            wire.left(r_h + 4 * mb + 2 * k, hp.at[0])
            wire.left(r_h + 4 * mb + 2 * k + 1, stat_src.at[0])
    for k in range(chips):
        wire.left(r_c + 2 * k, rc.at[0])
        wire.left(r_c + 2 * k + 1, rcs.at[0])
    for k in range(1, chips):
        wire.left(r_x + 2 * (k - 1), rx.at[0])
        wire.left(r_x + 2 * (k - 1) + 1, rxs.at[0])
    for k in range(1, ne):
        wire.left(r_z + 2 * (k - 1), rz.at[0])
        wire.left(r_z + 2 * (k - 1) + 1, rzs.at[0])
    assert wire.used <= BACK_ROLES


BACK_ROLES = 64


def back(nd, ne, *args):
    tokens = args[0]
    rows = tokens.shape[1]
    halo = -(-(IMG - 1) // 16) * 16
    chips = nd // 2
    part = D // nd
    share = part // ne
    shape = jax.ShapeDtypeStruct
    outs = (
        shape((MICRO, rows, D), bf16),
        shape((4, share, D), f32),
        shape((share, 128), f32),
        shape((2, D // nd, FF), f32),
        shape((2, FF // nd, D), f32),
    )
    vmem, anywhere = pl.BlockSpec(memory_space=pltpu.VMEM), pl.BlockSpec(memory_space=pl.ANY)
    v = pltpu.VMEM
    return pl.pallas_call(
        functools.partial(back_kernel, nd, ne),
        out_shape=outs,
        in_specs=[anywhere if k in (4, 5) else vmem for k in range(len(args))],
        out_specs=[vmem] * len(outs),
        scratch_shapes=[
            v((nd, D // nd, FF), bf16),
            v((nd, D, FF // nd), bf16),
            v((MICRO, rows, D), f32),
            v((MICRO, 3 * rows, D), bf16),
            v((MICRO, 2, HEADS, rows), f32),
            v((MICRO, 2, HEADS, rows), f32),
            v((MICRO, 2, HEADS, rows), f32),
            v((MICRO, halo, D), bf16),
            v((MICRO, halo, D), bf16),
            v((2, HEADS, 3 * rows), f32),
            v((rows, 3 * rows), f32),
            v((3, rows, D), bf16),
            v((4, D, D), f32),
            v((D, 128), f32),
            v((chips, 4, part, D), bf16),
            v((chips, part, 128), f32),
            v((chips, 4, part, D), bf16),
            v((chips, part, 128), f32),
            v((chips, 4, part, D), bf16),
            v((chips, part, 128), f32),
            v((chips, 4, part, D), bf16),
            v((chips, part, 128), f32),
            v((ne, 4, share, D), bf16),
            v((ne, share, 128), f32),
            v((ne, 4, share, D), bf16),
            v((ne, share, 128), f32),
            pltpu.SemaphoreType.DMA((BACK_ROLES,)),
            pltpu.SemaphoreType.DMA((BACK_ROLES,)),
            pltpu.SemaphoreType.DMA((2,)),
        ],
        compiler_params=pltpu.CompilerParams(
            collective_id=1, has_side_effects=True, vmem_limit_bytes=VMEM_BYTES
        ),
        name="back",
    )(*args)


def kernel_body(
    nd,
    ne,
    tokens,
    image_ids,
    routes,
    qkv_weight,
    out_weight,
    router_weight,
    norm_gains,
    norm_biases,
    expert_in,
    expert_out,
    cotangent,
):
    experts = 2 * ne
    small = jnp.concatenate([router_weight, norm_gains.T, norm_biases.T], axis=1)
    small = jnp.pad(small, ((0, 0), (0, 128 - experts - 4)))
    block_out, *saved = front(
        nd, ne, tokens, image_ids, routes, qkv_weight, out_weight, small, expert_in, expert_out, cotangent
    )
    input_grad, dense, small, grad_up, grad_down = back(nd, ne, tokens, cotangent, *saved)
    return (
        block_out,
        input_grad,
        dense[:3],
        dense[3],
        small[:, :experts],
        small[:, experts : experts + 2].T,
        small[:, experts + 2 : experts + 4].T,
        grad_up,
        grad_down,
    )


def chosen_body(nd, ne, tokens, *rest):
    rows, experts = tokens.shape[1], 2 * ne
    whole = D % (16 * nd * ne) == 0 and nd % 2 == 0 and 8 * rows == experts * rows and rows % 128 == 0
    if whole and rest[-3].shape[0] == 2:
        return kernel_body(nd, ne, tokens, *rest)
    return body(tokens, *rest)


def solution(mesh):
    return jax.shard_map(
        functools.partial(chosen_body, mesh.shape["dp"], mesh.shape["expert"]),
        mesh=mesh,
        in_specs=(
            P(None, ("dp", "expert"), None),
            P(None, ("dp", "expert")),
            P(None, ("dp", "expert"), None),
            P(None, ("dp", "expert"), None),
            P(("dp", "expert"), None),
            P(("dp", "expert"), None),
            P(None, ("dp", "expert")),
            P(None, ("dp", "expert")),
            P("expert", "dp", None),
            P("expert", "dp", None),
            P(None, ("dp", "expert"), None),
        ),
        out_specs=(
            P(None, ("dp", "expert"), None),
            P(None, ("dp", "expert"), None),
            P(None, ("dp", "expert"), None),
            P(("dp", "expert"), None),
            P(("dp", "expert"), None),
            P(None, ("dp", "expert")),
            P(None, ("dp", "expert")),
            P("expert", "dp", None),
            P("expert", "dp", None),
        ),
        check_vma=False,
    )
```

profile of v0, /device:TPU:0, one launch (start us, length us, event | category | flops | bytes accessed | tf_op | source)
XLA Modules:
  0.0 334.7 jit_solution(472279935643568478)
XLA Ops:
  0.6 0.8 copy.22
  1.4 0.7 copy.20
  2.1 0.7 copy.21
  2.9 0.7 fusion.4.small
  3.6 1.5 copy.23.routes
  5.1 240.5 %front.1 = (bf16[2,256,512]{2,1,0:T(8,128)(2,1)}, f32[2,256,512]{2,1,0:T(8,128)}, f32[2,256,128]{2,1,0:T(8,128)}, bf16[512,2048]{1,0:T(8,128)(2,1)}, bf16[512,20...) custom-call(bf16[2,256,512]{2,1,0:T(8,128)(2,1)} %tok.3, ...), custom_call_target="tpu_custom_call" | custom-call | tf_op jit(solution)/shard_map/front/pallas_call | solution.py:1164
  245.6 0.0 copy-start.2
  245.6 78.0 %back.1 = (bf16[2,256,512]{2,1,0:T(8,128)(2,1)}, f32[4,16,512]{2,1,0:T(8,128)}, f32[16,128]{1,0:T(8,128)}, f32[2,64,2048]{2,1,0:T(8,128)}, f32[2,256,512]{2,1,0:T(8,128)}) custom-call(bf16[2,256,512]{2,1,0:T(8,128)(2,1)} %tok.3, bf16[2,256,512]{2,1,0:T(8,128)(2,1)} %cot.3, f32[2,256,512]{2,1,0:T(8,128)} %get-tuple-element.29.d_in, ...), custom_call_target="tpu_custom_call" | custom-call | tf_op jit(solution)/shard_map/back/pallas_call | solution.py:1546
  323.6 0.0 copy-start.1
  323.6 1.4 copy.24
  325.0 0.8 slice_bitcast_fusion.1
  325.9 0.6 copy.26
  326.5 0.6 copy.25
  327.2 1.4 slice_bitcast_fusion
  328.5 1.5 slice.15
  330.1 0.0 copy-done.2
  330.1 0.0 copy-start
  330.1 0.8 copy.31
  330.9 1.9 copy.32
  332.7 0.0 copy-done.1
  332.7 1.0 copy.33
  333.7 0.0 copy-done
  333.7 1.0 copy.34
Async XLA Ops:
  245.6 84.5 %copy-start.2 = (bf16[2,256,512]{2,1,0:T(8,128)(2,1)S(1)}, bf16[2,256,512]{2,1,0:T(8,128)(2,1)}, u32[]{:S(2)}) copy-start(bf16[2,256,512]{2,1,0:T(8,128)(2,1)} %get-tuple-element.67) | copy-start | bytes 1572868
  323.6 9.2 %copy-start.1 = (f32[2,64,2048]{2,1,0:T(8,128)S(1)}, f32[2,64,2048]{2,1,0:T(8,128)}, u32[]{:S(2)}) copy-start(f32[2,64,2048]{2,1,0:T(8,128)} %get-tuple-element.74) | copy-start | bytes 3145732
  330.1 3.6 %copy-start = (f32[2,256,512]{2,1,0:T(8,128)S(1)}, f32[2,256,512]{2,1,0:T(8,128)}, u32[]{:S(2)}) copy-start(f32[2,256,512]{2,1,0:T(8,128)} %get-tuple-element.75) | copy-start | bytes 3145732
where the time goes:
time: 335 us
  Pallas kernels  318 us (95%)
  local copies, waits for them, and re-layouts  14.9 us (4%)
    pallas_call x1, Pallas kernels, front(): pl.pallas_call(functools.partial(front_kernel, nd, ne), out_shape=outs, i...  240 us
    pallas_call x1, Pallas kernels, back(): pl.pallas_call(functools.partial(back_kernel, nd, ne), out_shape=outs, in...  78 us
    unnamed x17, local copies, waits for them, and re-layouts  11.1 us

commit v1 on v0

--- a/solution.py
+++ b/solution.py
@@ -485,6 +485,8 @@
         first = (z == 0).astype(jnp.int32)
         self.next = (lax.rem(d + last, nd), lax.rem(z + 1, ne))
         self.prev = (lax.rem(d + nd - first, nd), lax.rem(z + ne - 1, ne))
+        self.xn = d + 2 - 4 * lax.rem(d // 2, 2)
+        self.yn = d + 4 - 8 * (d // 4)
         self.up = (d, jnp.minimum(z + 1, ne - 1))
         self.down = (d, jnp.maximum(z - 1, 0))
 
@@ -558,18 +560,19 @@
 
             w.send(self.sd + k, block, block, m.sib)
 
-    def finish(self):
+    def near(self):
+        self.wire.arrive(self.so, self.full.at[0])
+
+    def finish(self, k):
         m, n, w, like = self.me, self.me.ne, self.wire, self.full.at[0]
-        w.arrive(self.so, like)
-        for k in range(n - 1):
-
-            @pl.when(m.z >= k + 1)
-            def _():
-                w.arrive(self.su + k, like)
-
-            @pl.when(m.z + k + 1 < n)
-            def _():
-                w.arrive(self.sd + k, like)
+
+        @pl.when(m.z >= k + 1)
+        def _():
+            w.arrive(self.su + k, like)
+
+        @pl.when(m.z + k + 1 < n)
+        def _():
+            w.arrive(self.sd + k, like)
 
     def drain(self):
         m, n, w, like = self.me, self.me.ne, self.wire, self.full.at[0]
@@ -601,12 +604,14 @@
     routes,
     qkv,
     outw,
-    small,
+    routw,
+    gainw,
+    biasw,
     win,
     wout,
     cot,
-    o_block,
     o_din,
+    o_y,
     o_dprobs,
     o_up,
     o_down,
@@ -631,10 +636,9 @@
     wd,
     rk_src,
     rk,
-    hnorm,
     bias,
-    d_wu,
-    d_wd,
+    acts,
+    grads,
     pm,
     xs,
     ds,
@@ -651,6 +655,8 @@
     ud,
     dgs,
     dg,
+    stage,
+    square,
     send_sems,
     recv_sems,
     local_sems,
@@ -665,6 +671,7 @@
     slots = 4 * rows // experts
     capacity = 5 * TOP * rows * nd * ne // (4 * experts)
     e = 2 * z + c
+    s_me = z * 2 + c
     wire = Wire(send_sems, recv_sems, me.sib)
     lane = lax.broadcasted_iota(jnp.int32, (1, 128), 1)
 
@@ -672,13 +679,19 @@
         lax.broadcasted_iota(jnp.int32, (rows, rows), 0)
         > lax.broadcasted_iota(jnp.int32, (rows, rows), 1)
     ).astype(bf16)
+    square[...] = jnp.zeros_like(square)
+    square[0:experts, 0:share] = routw[...].astype(f32)
+    square[experts : experts + 2, 0:share] = gainw[...].astype(f32)
+    square[experts + 2 : experts + 4, 0:share] = biasw[...].astype(f32)
+    s_src[0:share, :] = square[...].T[0:share, :].astype(bf16)
+    row128 = lax.broadcasted_iota(jnp.int32, (128, rows), 0)
+    row16 = lax.broadcasted_iota(jnp.int32, (16, 128), 0)
     hots = []
-    s_src[0:share, :] = small[...]
-    s_src[share : share + 16, :] = jnp.zeros((16, 128), bf16)
-    row16 = lax.broadcasted_iota(jnp.int32, (16, 128), 0)
     counts = jnp.zeros((16, 128), f32)
     for mb in range(MICRO):
-        pair = [(routes[mb, :, k : k + 1] == lane).astype(f32) for k in range(TOP)]
+        choice = routes[mb].astype(f32)
+        wide = jnp.where(row128 == 0, choice[0:1], jnp.where(row128 == 1, choice[1:2], -1.0)).T
+        pair = [(wide[:, k : k + 1] == lane.astype(f32)).astype(f32) for k in range(TOP)]
         hots.append(pair)
         for k in range(TOP):
             counts = jnp.where(row16 == mb * TOP + k, jnp.sum(pair[k], axis=0, keepdims=True), counts)
@@ -700,22 +713,43 @@
     ]
     for cp in local:
         cp.start()
+    up_rows, down_rows = win.shape[1], wout.shape[1]
+
+    def up_at(dd, n=1):
+        return wu.at[pl.ds(pl.multiple_of(dd * up_rows, 16), n * up_rows)]
+
+    def down_at(dd, n=1):
+        return wd.at[pl.ds(pl.multiple_of(dd * down_rows, 16), n * down_rows)]
+
+    own_w = [
+        pltpu.make_async_copy(win.at[c], up_at(d), local_sems.at[5]),
+        pltpu.make_async_copy(wout.at[c], down_at(d), local_sems.at[6]),
+    ]
+    for cp in own_w:
+        cp.start()
+    r_ux, r_dy, r_uy, r_dx2 = (wire.roles(2) for _ in range(4))
+    r_uf, r_df, r_us, r_dsib = (wire.roles() for _ in range(4))
+    for cc in range(2):
+        wire.send(r_ux + cc, win.at[cc], up_at(d), (me.xn - c + cc, z), recv_role=r_ux + c)
+        wire.send(r_dy + cc, wout.at[cc], down_at(d), (me.yn - c + cc, z), recv_role=r_dy + c)
     r_id = wire.roles(2)
     wire.send(r_id, ids, ip, me.next)
     wire.send(r_id + 1, ids, inx, me.prev)
     r_h = wire.roles(2 * MICRO)
-    for mb in range(MICRO):
+
+    def send_halo(mb):
         wire.send(r_h + 2 * mb, tok.at[mb, pl.ds(rows - halo, halo)], hp.at[mb], me.next)
         wire.send(r_h + 2 * mb + 1, tok.at[mb, pl.ds(0, halo)], hn.at[mb], me.prev)
+
+    send_halo(0)
     g_d = [Chain(wire, me, gd.at[mb]) for mb in range(MICRO)]
     g_x = [Chain(wire, me, gx.at[mb]) for mb in range(MICRO)]
     own_d = [
-        pltpu.make_async_copy(cot.at[mb], gd.at[mb, z * 2 + c], local_sems.at[3 + mb])
+        pltpu.make_async_copy(cot.at[mb], gd.at[mb, s_me], local_sems.at[3 + mb])
         for mb in range(MICRO)
     ]
     for cp in own_d:
         cp.start()
-    g_d[0].own(cot.at[0])
 
     for cp in local:
         cp.wait()
@@ -737,28 +771,23 @@
         wire.send(r_dx + 2 * (k - 1) + 1, sblk, sblk, (me.chip(k), z))
     wire.send(r_ds, blk, blk, me.sib)
     wire.send(r_ds + 1, sblk, sblk, me.sib)
-    up_rows, down_rows = win.shape[1], wout.shape[1]
-    at_up = pl.ds(pl.multiple_of(d * up_rows, 16), up_rows)
-    at_down = pl.ds(pl.multiple_of(d * down_rows, 16), down_rows)
-    r_w = wire.roles(2 * (nd - 1))
-    own_w = [
-        pltpu.make_async_copy(win.at[c], wu.at[at_up], local_sems.at[5]),
-        pltpu.make_async_copy(wout.at[c], wd.at[at_down], local_sems.at[6]),
-    ]
-    for cp in own_w:
-        cp.start()
-    for k in range(1, nd):
-        dd = lax.rem(d + k, nd)
-        cc = lax.rem(dd, 2)
-        wire.send(r_w + 2 * (k - 1), win.at[cc], wu.at[at_up], (dd, z))
-        wire.send(r_w + 2 * (k - 1) + 1, wout.at[cc], wd.at[at_down], (dd, z))
-    g_d[0].pump(0)
+    send_halo(1)
+    g_d[0].own(cot.at[0])
+    wire.send(r_us, win.at[1 - c], up_at(d), me.sib)
+    wire.send(r_dsib, wout.at[1 - c], down_at(d), me.sib)
     for k in range(1, chips):
         wire.arrive(r_dx + 2 * (k - 1), blk)
         wire.arrive(r_dx + 2 * (k - 1) + 1, sblk)
         b, sb = column(lax.rem(d + nd - 2 * k, nd))
         wire.send(r_ds + 2 * k, b, b, me.sib)
         wire.send(r_ds + 2 * k + 1, sb, sb, me.sib)
+    for cc in range(2):
+        wire.send(r_dx2 + cc, wout.at[cc], down_at(d), (me.xn - c + cc, z), recv_role=r_dx2 + c)
+        wire.send(r_uy + cc, win.at[cc], up_at(d), (me.yn - c + cc, z), recv_role=r_uy + c)
+        wire.arrive(r_ux + cc, win.at[0])
+        wire.arrive(r_dy + cc, wout.at[0])
+    wire.send(r_uf, up_at(me.xn - c, 2), up_at(me.xn - c, 2), (me.yn, z))
+    wire.send(r_df, down_at(me.yn - c, 2), down_at(me.yn - c, 2), (me.xn, z))
     for k in range(chips):
         wire.arrive(r_ds + 2 * k, blk)
         wire.arrive(r_ds + 2 * k + 1, sblk)
@@ -772,26 +801,28 @@
     gains = [s_rows[experts + k : experts + k + 1, :] for k in range(2)]
     biases = [s_rows[experts + 2 + k : experts + 3 + k, :] for k in range(2)]
 
-    for mb in range(MICRO):
-        one, two = hots[mb]
-        rank_one = mm(before_row, one.astype(bf16))
-        rank_two = mm(before_row, two.astype(bf16))
-        b1, b2 = before[2 * mb : 2 * mb + 1], before[2 * mb + 1 : 2 * mb + 2]
-        t1 = total[2 * mb : 2 * mb + 1]
-        place_one = jnp.sum(one * (b1 + rank_one), axis=1, keepdims=True)
-        place_two = jnp.sum(two * (t1 + b2 + rank_two), axis=1, keepdims=True)
-        kept = one * (place_one < capacity).astype(f32) + two * (place_two < capacity).astype(f32)
-        ranks = jnp.where(kept > 0.0, rank_one + rank_two, -1.0)
-        rk_src[mb] = ranks.T[0:experts, :]
     r_rk = wire.roles(2 * ne)
-    s_me = z * 2 + c
-    for k in range(ne):
-        zk = lax.rem(z + k, ne)
-        if k > 0:
-            wire.send(r_rk + 2 * k, rk_src, rk.at[s_me], (d, zk))
-        wire.send(r_rk + 2 * k + 1, rk_src, rk.at[s_me], (me.sib_d, zk))
-    rk[s_me] = rk_src[...]
-    g_d[0].pump(1)
+
+    def send_ranks():
+        for mb in range(MICRO):
+            one, two = hots[mb]
+            rank_one = mm(before_row, one.astype(bf16))
+            rank_two = mm(before_row, two.astype(bf16))
+            b1, b2 = before[2 * mb : 2 * mb + 1], before[2 * mb + 1 : 2 * mb + 2]
+            t1 = total[2 * mb : 2 * mb + 1]
+            place_one = jnp.sum(one * (b1 + rank_one), axis=1, keepdims=True)
+            place_two = jnp.sum(two * (t1 + b2 + rank_two), axis=1, keepdims=True)
+            kept = one * (place_one < capacity).astype(f32) + two * (place_two < capacity).astype(
+                f32
+            )
+            ranks = jnp.where(kept > 0.0, rank_one + rank_two, -1.0)
+            rk_src[mb] = ranks.T[0:experts, :]
+        for k in range(ne):
+            zk = lax.rem(z + k, ne)
+            if k > 0:
+                wire.send(r_rk + 2 * k, rk_src, rk.at[s_me], (d, zk))
+            wire.send(r_rk + 2 * k + 1, rk_src, rk.at[s_me], (me.sib_d, zk))
+        rk[s_me] = rk_src[...]
 
     wire.arrive(r_id, ids)
     wire.arrive(r_id + 1, ids)
@@ -806,26 +837,33 @@
         o_idr[mb] = jnp.concatenate([below, here, above], axis=1)
 
     zero_gap = jnp.zeros((gap, D), bf16)
-    hnorm[0:gap, :] = zero_gap
-    hnorm[ext - gap : ext, :] = zero_gap
+    acts[0:gap, 0:D] = zero_gap
+    acts[ext - gap : ext, 0:D] = zero_gap
     scale = 1.0 / math.sqrt(HEAD_DIM)
-    for mb in range(MICRO):
+    saves = [pltpu.make_async_copy(
+            acts.at[pl.ds(0, ext), pl.ds(D, 3 * D)], o_qkv.at[mb], local_sems.at[7 + mb]
+        )
+        for mb in range(MICRO)]
+
+    def attend(mb, hooks):
         wire.arrive(r_h + 2 * mb, hp.at[mb])
         wire.arrive(r_h + 2 * mb + 1, hn.at[mb])
 
         def put(value, start):
-            hnorm[start : start + value.shape[0], :] = normed(
+            acts[start : start + value.shape[0], 0:D] = normed(
                 value.astype(f32), gains[0], biases[0]
             ).astype(bf16)
 
         put(hp[mb], gap)
         put(tok[mb], rows)
         put(hn[mb], 2 * rows)
+        if mb > 0:
+            saves[mb - 1].wait()
         for k in range(3):
             for r in range(3):
                 part = slice(r * rows, (r + 1) * rows)
-                o_qkv[mb, k, part, :] = mm(hnorm[part, :], w_all[k]).astype(bf16)
-        g_d[0].pump(2) if mb == 0 else g_x[0].pump(0)
+                acts[part, (k + 1) * D : (k + 2) * D] = mm(acts[part, 0:D], w_all[k]).astype(bf16)
+        saves[mb].start()
         idr = o_idr[mb]
         idc = jnp.broadcast_to(idr[:, rows : 2 * rows], (128, rows)).T[:, 0:1]
         bias[...] = jnp.where(idc == idr, 0.0, neg_big)
@@ -834,9 +872,10 @@
         @pl.loop(0, HEADS // 2)
         def _(pair):
             at = pl.ds(pl.multiple_of(pair * 128, 128), 128)
-            query = o_qkv[mb, 0, rows : 2 * rows, at]
-            key = o_qkv[mb, 1, :, at]
-            value = o_qkv[mb, 2, :, at]
+            query, key, value = (
+                acts[part, pl.ds(pl.multiple_of((k + 1) * D + pair * 128, 128), 128)]
+                for k, part in enumerate((slice(rows, 2 * rows), slice(0, ext), slice(0, ext)))
+            )
             mixed = jnp.zeros((rows, 128), f32)
             lse = o_lse[mb]
             for half in range(2):
@@ -851,123 +890,156 @@
                 lse = jnp.where(lane == 2 * pair + half, top + jnp.log(total_p), lse)
             o_lse[mb] = lse
             o_mixed[mb, :, at] = mixed.astype(bf16)
-
-        if mb == 1:
-            g_x[0].pump(1)
+            for when, hook in hooks.items():
+                pl.when(pair == when)(hook)
+
         resid = tok[mb].astype(f32) + mm(o_mixed[mb], w_all[3])
         o_resid[mb] = resid
         n2 = normed(resid, gains[1], biases[1]).astype(bf16)
         o_n2[mb] = n2
         gx[mb, s_me] = n2
         g_x[mb].own(gx.at[mb, s_me])
-        if mb == 0:
-            g_d[1].own(cot.at[1])
         logits = mm(n2, o_small[...].astype(bf16))
         logits = jnp.where(lane < experts, logits, neg_big)
         p = jnp.exp(logits - jnp.max(logits, axis=-1, keepdims=True))
         o_probs[mb] = p / jnp.sum(p, axis=-1, keepdims=True)
-    g_x[0].pump(2)
-
-    for cp in own_w + own_d:
-        cp.wait()
-    for k in range(1, nd):
-        wire.arrive(r_w + 2 * (k - 1), win.at[0])
-        wire.arrive(r_w + 2 * (k - 1) + 1, wout.at[0])
-    for k in range(ne):
-        if k > 0:
-            wire.arrive(r_rk + 2 * k, rk_src)
-        wire.arrive(r_rk + 2 * k + 1, rk_src)
-    g_d[0].finish()
-    g_x[0].finish()
-    d_wu[...] = jnp.zeros_like(d_wu)
-    d_wd[...] = jnp.zeros_like(d_wd)
+
+    def later_halves():
+        g_x[0].pump(0)
+        g_d[1].own(cot.at[1])
+
+    attend(0, {0: lambda: g_d[0].pump(0), 3: lambda: g_d[0].pump(1)})
+    send_ranks()
+    attend(1, {0: lambda: g_d[0].pump(2), 2: later_halves})
+    g_x[0].pump(1)
 
     r_cx = wire.roles(2 * MICRO * ne)
-    r_up = wire.roles(2 * MICRO * ne)
-    r_dn = wire.roles(2 * MICRO * ne)
+    r_up = wire.roles(MICRO * ne)
+    r_dn = wire.roles(MICRO * ne)
     r_dg = wire.roles(MICRO * 2 * ne)
     sub = lax.broadcasted_iota(jnp.int32, (slots, rows), 0).astype(f32)
     tile = 2 * slots
     chunk = 512
-
-    def start_sums(mb):
+    like = qo.at[0, 0, 0]
+
+    def target(i):
+        swap = jnp.where(i < 2, 1 - i, i)
+        return jnp.where(
+            z == 0, i, jnp.where(z == 1, swap, jnp.where(z == 2, ne - 1 - swap, ne - 1 - i))
+        )
+
+    def pass_up(mb, to):
+        wire.send(r_up + mb * ne + to, qo.at[mb, 0, to], ud.at[mb, to], me.up)
+
+    def pass_down(mb, to):
+        slot = jnp.where(z - 1 == to, ne, to)
+        wire.send(r_dn + mb * ne + to, qo.at[mb, 0, to], ud.at[mb, slot], me.down)
+
+    def settle(mb, zp):
         for t in range(2):
-            for zp in range(ne):
-                wire.arrive(r_cx + (mb * 2 + t) * ne + zp, qo.at[0, 0, 0])
-                qo[mb, t, zp] = (qo[mb, t, zp].astype(f32) + cr[mb, t, zp].astype(f32)).astype(bf16)
-
-        @pl.when(z == 0)
-        def _():
-            for t in range(2):
-                for to in range(ne - 1, 0, -1):
-                    wire.send(
-                        r_up + (mb * 2 + t) * ne + to, qo.at[mb, t, to], ud.at[mb, t, to], me.up
-                    )
-
-        @pl.when(z == ne - 1)
-        def _():
-            for t in range(2):
-                for to in range(ne - 1):
-                    slot = jnp.where(z - 1 == to, ne, to)
-                    wire.send(
-                        r_dn + (mb * 2 + t) * ne + to, qo.at[mb, t, to], ud.at[mb, t, slot], me.down
-                    )
-
-    def pass_sums(mb):
-        for t in range(2):
-            for k in range(ne - 1):
-                to = ne - 1 - k
-
-                @pl.when((z > 0) & (z < to))
-                def _():
-                    wire.arrive(r_up + (mb * 2 + t) * ne + to, qo.at[0, 0, 0])
-                    qo[mb, t, to] = (
-                        qo[mb, t, to].astype(f32) + ud[mb, t, to].astype(f32)
-                    ).astype(bf16)
-                    wire.send(
-                        r_up + (mb * 2 + t) * ne + to, qo.at[mb, t, to], ud.at[mb, t, to], me.up
-                    )
-
-                @pl.when((z < ne - 1) & (z > k))
-                def _():
-                    wire.arrive(r_dn + (mb * 2 + t) * ne + k, qo.at[0, 0, 0])
-                    qo[mb, t, k] = (
-                        qo[mb, t, k].astype(f32) + ud[mb, t, k].astype(f32)
-                    ).astype(bf16)
-                    slot = jnp.where(z - 1 == k, ne, k)
-                    wire.send(
-                        r_dn + (mb * 2 + t) * ne + k, qo.at[mb, t, k], ud.at[mb, t, slot], me.down
-                    )
-
-    def end_sums(mb, t):
-        out = qo[mb, t, z].astype(f32)
-        acc_eo[...] = out
+            wire.arrive(r_cx + (mb * 2 + t) * ne + zp, like)
+            qo[mb, t, zp] = (qo[mb, t, zp].astype(f32) + cr[mb, t, zp].astype(f32)).astype(bf16)
+
+        @pl.when((z == 0) & (zp > 0))
+        def _():
+            pass_up(mb, zp)
+
+        @pl.when((z == ne - 1) & (zp < ne - 1))
+        def _():
+            pass_down(mb, zp)
+
+    def relay(mb, hop, to):
+        @pl.when(z == hop)
+        def _():
+            wire.arrive(r_up + mb * ne + to, like)
+            qo[mb, 0, to] = (qo[mb, 0, to].astype(f32) + ud[mb, to].astype(f32)).astype(bf16)
+            pass_up(mb, to)
+
+        @pl.when(z == ne - 1 - hop)
+        def _():
+            low = ne - 1 - to
+            wire.arrive(r_dn + mb * ne + low, like)
+            qo[mb, 0, low] = (qo[mb, 0, low].astype(f32) + ud[mb, low].astype(f32)).astype(bf16)
+            pass_down(mb, low)
+
+    def end_sums(mb):
+        acc_eo[...] = qo[mb, 0, z].astype(f32)
 
         @pl.when(z > 0)
         def _():
-            wire.arrive(r_up + (mb * 2 + t) * ne + z, qo.at[0, 0, 0])
-            acc_eo[...] += ud[mb, t, z].astype(f32)
+            wire.arrive(r_up + mb * ne + z, like)
+            acc_eo[...] += ud[mb, z].astype(f32)
 
         @pl.when(z < ne - 1)
         def _():
-            wire.arrive(r_dn + (mb * 2 + t) * ne + z, qo.at[0, 0, 0])
-            acc_eo[...] += ud[mb, t, ne].astype(f32)
-
-        return acc_eo[...]
+            wire.arrive(r_dn + mb * ne + z, like)
+            acc_eo[...] += ud[mb, ne].astype(f32)
+
+        o_din[mb] = acc_eo[...]
+
+    def first_tile():
+        for cp in own_w + own_d + saves[1:]:
+            cp.wait()
+        for cc in range(2):
+            wire.arrive(r_uy + cc, win.at[0])
+            wire.arrive(r_dx2 + cc, wout.at[0])
+        wire.arrive(r_us, win.at[0])
+        wire.arrive(r_dsib, wout.at[0])
+        wire.arrive(r_uf, up_at(0, 2))
+        wire.arrive(r_df, down_at(0, 2))
+        for k in range(ne):
+            if k > 0:
+                wire.arrive(r_rk + 2 * k, rk_src)
+            wire.arrive(r_rk + 2 * k + 1, rk_src)
+        g_d[0].near()
+        g_x[0].near()
+
+    def both(mb, what, k):
+        for g in (g_d[mb], g_x[mb]):
+            getattr(g, what)(k)
+
+    def tile_1():
+        both(0, "finish", 0)
+        g_x[0].pump(2)
+
+    def tile_2():
+        both(0, "finish", 1)
+
+    def tile_3():
+        both(0, "finish", 2)
+        both(1, "pump", 0)
+
+    def tile_4():
+        g_d[1].near()
+        g_x[1].near()
+
+    def tile_5():
+        both(1, "finish", 0)
+        both(1, "pump", 1)
+        relay(0, 1, 2)
+
+    def tile_6():
+        both(1, "finish", 1)
+        both(1, "pump", 2)
+        relay(0, 1, 3)
+
+    def tile_7():
+        both(1, "finish", 2)
+        relay(0, 2, 3)
+
+    before_tile = [first_tile, tile_1, tile_2, tile_3, tile_4, tile_5, tile_6, tile_7]
 
     @pl.loop(0, MICRO * ne)
     def _(i):
-        mb, zi = i // ne, lax.rem(i, ne)
-        zp = lax.rem(zi * (ne - 1), ne)
-
-        @pl.when(i == ne)
-        def _():
-            start_sums(0)
-            for k in range(ne - 1):
-                g_d[1].pump(k)
-                g_x[1].pump(k)
-            g_d[1].finish()
-            g_x[1].finish()
+        mb = i // ne
+        zp = target(lax.rem(i, ne))
+
+        @pl.when(i > 0)
+        def _():
+            settle((i - 1) // ne, target(lax.rem(i - 1 + ne, ne)))
+
+        for when, hook in enumerate(before_tile):
+            pl.when(i == when)(hook)
 
         for cc in range(2):
             s = zp * 2 + cc
@@ -985,8 +1057,9 @@
         gt[...] = jnp.broadcast_to(gate, (tile, 128))
         dy = (gate * ds[...].astype(f32)).astype(bf16)
         deo[...] = dy
-        xt[...] = x.T
-        dt[...] = dy.T
+        across = pl.ds(pl.multiple_of(i * tile, tile), tile)
+        xt[:, across] = x.T
+        dt[:, across] = dy.T
         acc_eo[...] = jnp.zeros_like(acc_eo)
         acc_di[...] = jnp.zeros_like(acc_di)
 
@@ -994,23 +1067,31 @@
         def _(f):
             at = pl.ds(pl.multiple_of(f * chunk, chunk), chunk)
             pre = mm(xs[...], wu[:, at])
+            d_act = mm_nt(deo[...], wd[at, :])
             sq = pre * pre
             k0 = math.sqrt(2.0 / math.pi)
             th = jnp.tanh(pre * (k0 + (k0 * 0.044715) * sq))
             half = 0.5 + 0.5 * th
             act = (pre * half).astype(bf16)
             slope = half + (0.5 * pre) * (1.0 - th * th) * (k0 + (3.0 * k0 * 0.044715) * sq)
+            d_pre = (slope * d_act).astype(bf16)
+            acts[across, at] = act
+            grads[across, at] = d_pre
             acc_eo[...] += mm(act, wd[at, :])
-            d_act = mm_nt(deo[...], wd[at, :])
-            d_pre = (slope * d_act).astype(bf16)
             acc_di[...] += mm_nt(d_pre, wu[:, at])
-            d_wu[:, at] += mm(xt[...], d_pre)
-            d_wd[:, at] += mm(dt[...], act)
 
         eo = acc_eo[...].astype(bf16).astype(f32)
         d_gate = jnp.sum(ds[...].astype(f32) * eo, axis=-1, keepdims=True)
         ys[0] = acc_di[...].astype(bf16)
         ys[1] = (gt[:, 0:1] * eo).astype(bf16)
+        box = lax.rem(i, 2)
+
+        @pl.when(i > 1)
+        def _():
+            old = i - 2
+            for t in range(2):
+                wire.left(r_cx + ((old // ne) * 2 + t) * ne + target(lax.rem(old, ne)), like)
+
         for own in range(2):
             cc = c if own else 1 - c
             back = pm[cc].T
@@ -1020,10 +1101,10 @@
                 if own:
                     qo[mb, t, zp] = moved
                 else:
-                    cs[mb, t, zp] = moved
+                    cs[box, t] = moved
         for t in range(2):
             role = r_cx + (mb * 2 + t) * ne + zp
-            wire.send(role, cs.at[mb, t, zp], cr.at[mb, t, zp], me.sib)
+            wire.send(role, cs.at[box, t], cr.at[mb, t, zp], me.sib)
         for cc in range(2):
             at = slice(cc * slots, (cc + 1) * slots)
             line = jnp.sum(pm[cc].astype(f32) * d_gate[at], axis=0, keepdims=True)
@@ -1044,28 +1125,25 @@
             def _():
                 dg[mb, e] = jnp.broadcast_to(line, (8, rows))
 
-    pass_sums(0)
-    start_sums(1)
-    g_d[0].drain()
-    out_copies = []
-    for h in range(2):
-        for q in range(4):
-            at = (slice(h * 256, (h + 1) * 256), slice(q * chunk, (q + 1) * chunk))
-            wu[at] = d_wu[at].astype(bf16)
-            gd[0, h * 4 + q] = d_wd[at].astype(bf16)
-            to = o_down.at[pl.ds(h * 256, 256), pl.ds(q * chunk, chunk)]
-            out_copies.append(pltpu.make_async_copy(gd.at[0, h * 4 + q], to, local_sems.at[h * 4 + q]))
-    out_copies.append(pltpu.make_async_copy(wu, o_up, local_sems.at[8]))
-    for cp in out_copies:
+    settle(1, target(ne - 1))
+
+    wide_at = [pl.ds(k * chunk, chunk) for k in range(FF // chunk)]
+    outs = []
+    hooks = {0: lambda: relay(1, 1, 2), 1: lambda: relay(1, 1, 3), 3: lambda: relay(1, 2, 3)}
+    for f, at in enumerate(wide_at):
+        for k, (left, right, to) in enumerate(((xt, grads, o_up), (dt, acts, o_down))):
+            if f > 1:
+                outs[2 * (f - 2) + k].wait()
+            stage[f % 2, k] = mm(left[...], right[:, at]).astype(bf16)
+            cp = pltpu.make_async_copy(stage.at[f % 2, k], to.at[:, at], local_sems.at[9 + 2 * f + k])
+            cp.start()
+            outs.append(cp)
+        if f in hooks:
+            hooks[f]()
+    end_sums(0)
+    give_y = [pltpu.make_async_copy(qo.at[mb, 1], o_y.at[mb], local_sems.at[mb]) for mb in range(MICRO)]
+    for cp in give_y:
         cp.start()
-
-    def outputs(mb):
-        o_din[mb] = end_sums(mb, 0)
-        o_block[mb] = (o_resid[mb] + end_sums(mb, 1)).astype(bf16)
-
-    outputs(0)
-    pass_sums(1)
-    outputs(1)
     for mb in range(MICRO):
         for s in range(2 * ne):
 
@@ -1082,9 +1160,10 @@
             groups.append(group)
         lines = jnp.concatenate(groups + [jnp.zeros((128 - experts, rows), f32)], axis=0)
         o_dprobs[mb] = lines.T
-
-    for cp in out_copies:
+    end_sums(1)
+    for cp in outs[-4:] + give_y:
         cp.wait()
+
     for k in range(1, ne):
         wire.left(r_dz + 3 * (k - 1), qkv)
         wire.left(r_dz + 3 * (k - 1) + 1, outw)
@@ -1099,31 +1178,36 @@
     for k in range(chips):
         wire.left(r_ds + 2 * k, blk)
         wire.left(r_ds + 2 * k + 1, sblk)
-    for k in range(1, nd):
-        wire.left(r_w + 2 * (k - 1), win.at[0])
-        wire.left(r_w + 2 * (k - 1) + 1, wout.at[0])
+    for cc in range(2):
+        wire.left(r_ux + cc, win.at[0])
+        wire.left(r_uy + cc, win.at[0])
+        wire.left(r_dy + cc, wout.at[0])
+        wire.left(r_dx2 + cc, wout.at[0])
+    wire.left(r_us, win.at[0])
+    wire.left(r_dsib, wout.at[0])
+    wire.left(r_uf, up_at(0, 2))
+    wire.left(r_df, down_at(0, 2))
     for k in range(ne):
         if k > 0:
             wire.left(r_rk + 2 * k, rk_src)
         wire.left(r_rk + 2 * k + 1, rk_src)
-    for g in [g_d[1]] + g_x:
+    for g in g_d + g_x:
         g.drain()
+    for old in (MICRO * ne - 2, MICRO * ne - 1):
+        for t in range(2):
+            wire.left(r_cx + ((old // ne) * 2 + t) * ne + target(old % ne), like)
     for mb in range(MICRO):
-        for t in range(2):
-            base = (mb * 2 + t) * ne
-            for zp in range(ne):
-                wire.left(r_cx + base + zp, qo.at[0, 0, 0])
-            for to in range(1, ne):
-
-                @pl.when(z < to)
-                def _():
-                    wire.left(r_up + base + to, qo.at[0, 0, 0])
-
-            for to in range(ne - 1):
-
-                @pl.when(z > to)
-                def _():
-                    wire.left(r_dn + base + to, qo.at[0, 0, 0])
+        for to in range(1, ne):
+
+            @pl.when(z < to)
+            def _():
+                wire.left(r_up + mb * ne + to, like)
+
+        for to in range(ne - 1):
+
+            @pl.when(z > to)
+            def _():
+                wire.left(r_dn + mb * ne + to, like)
 
         for s in range(2 * ne):
 
@@ -1134,38 +1218,41 @@
     assert wire.used <= ROLES
 
 
-ROLES = 240
-
-
-def front(nd, ne, tokens, image_ids, routes, qkv, outw, small, win, wout, cot):
+ROLES = 192
+
+
+def front(nd, ne, *args):
+    tokens, qkv = args[0], args[3]
     rows, share = tokens.shape[1], qkv.shape[1]
     halo = -(-(IMG - 1) // 16) * 16
     experts = 2 * ne
     slots = 4 * rows // experts
+    tile = 2 * slots
+    every = MICRO * ne * tile
     shape = jax.ShapeDtypeStruct
+    vmem, anywhere = pl.BlockSpec(memory_space=pltpu.VMEM), pl.BlockSpec(memory_space=pl.ANY)
     outs = (
-        shape((MICRO, rows, D), bf16),
-        shape((MICRO, rows, D), f32),
-        shape((MICRO, rows, 128), f32),
-        shape((D, FF), bf16),
-        shape((D, FF), bf16),
-        shape((MICRO, rows, D), bf16),
-        shape((MICRO, rows, 128), f32),
-        shape((MICRO, rows, D), f32),
-        shape((MICRO, rows, D), bf16),
-        shape((MICRO, 3, 3 * rows, D), bf16),
-        shape((MICRO, rows, 128), f32),
-        shape((4, D, D), bf16),
-        shape((D, 128), f32),
-        shape((MICRO, 1, 3 * rows), f32),
-    )
-    vmem, anywhere = pl.BlockSpec(memory_space=pltpu.VMEM), pl.BlockSpec(memory_space=pl.ANY)
+        (vmem, (MICRO, rows, D), f32),
+        (anywhere, (MICRO, ne, rows, D), bf16),
+        (vmem, (MICRO, rows, 128), f32),
+        (anywhere, (D, FF), bf16),
+        (anywhere, (D, FF), bf16),
+        (vmem, (MICRO, rows, D), bf16),
+        (vmem, (MICRO, rows, 128), f32),
+        (vmem, (MICRO, rows, D), f32),
+        (vmem, (MICRO, rows, D), bf16),
+        (anywhere, (MICRO, 3 * rows, 3 * D), bf16),
+        (vmem, (MICRO, rows, 128), f32),
+        (vmem, (4, D, D), bf16),
+        (vmem, (D, 128), f32),
+        (vmem, (MICRO, 1, 3 * rows), f32),
+    )
     v = pltpu.VMEM
     return pl.pallas_call(
         functools.partial(front_kernel, nd, ne),
-        out_shape=outs,
-        in_specs=[vmem, vmem, vmem, anywhere, anywhere, vmem, anywhere, anywhere, anywhere],
-        out_specs=[anywhere if k in (3, 4) else vmem for k in range(len(outs))],
+        out_shape=[shape(*o[1:]) for o in outs],
+        in_specs=[vmem, vmem, vmem, anywhere, anywhere, vmem, vmem, vmem] + [anywhere] * 3,
+        out_specs=[o[0] for o in outs],
         scratch_shapes=[
             v((share + 16, 128), bf16),
             v((nd * ne, share + 16, 128), bf16),
@@ -1179,35 +1266,36 @@
             v((FF, D), bf16),
             v((MICRO, experts, rows), f32),
             v((2 * ne, MICRO, experts, rows), f32),
-            v((3 * rows, D), bf16),
             v((rows, 3 * rows), f32),
-            v((D, FF), f32),
-            v((D, FF), f32),
+            v((every, FF), bf16),
+            v((every, FF), bf16),
             v((2, slots, rows), bf16),
-            v((2 * slots, D), bf16),
-            v((2 * slots, D), bf16),
-            v((2 * slots, D), bf16),
-            v((D, 2 * slots), bf16),
-            v((D, 2 * slots), bf16),
-            v((2 * slots, 128), f32),
-            v((2 * slots, D), f32),
-            v((2 * slots, D), f32),
-            v((2, 2 * slots, D), bf16),
+            v((tile, D), bf16),
+            v((tile, D), bf16),
+            v((tile, D), bf16),
+            v((D, every), bf16),
+            v((D, every), bf16),
+            v((tile, 128), f32),
+            v((tile, D), f32),
+            v((tile, D), f32),
+            v((2, tile, D), bf16),
             v((MICRO, 2, ne, rows, D), bf16),
+            v((2, 2, rows, D), bf16),
             v((MICRO, 2, ne, rows, D), bf16),
-            v((MICRO, 2, ne, rows, D), bf16),
-            v((MICRO, 2, ne + 1, rows, D), bf16),
+            v((MICRO, ne + 1, rows, D), bf16),
             v((MICRO, 2 * ne, 8, rows), f32),
             v((MICRO, experts, 8, rows), f32),
+            v((2, 2, D, 512), bf16),
+            v((128, 128), f32),
             pltpu.SemaphoreType.DMA((ROLES,)),
             pltpu.SemaphoreType.DMA((ROLES,)),
-            pltpu.SemaphoreType.DMA((9,)),
+            pltpu.SemaphoreType.DMA((17,)),
         ],
         compiler_params=pltpu.CompilerParams(
             collective_id=0, has_side_effects=True, vmem_limit_bytes=VMEM_BYTES
         ),
         name="front",
-    )(tokens, image_ids, routes, qkv, outw, small, win, wout, cot)
+    )(*args)
 
 
 def mm_exact(a, b):
@@ -1220,6 +1308,7 @@
     tok,
     cot,
     d_in,
+    y,
     d_probs,
     up,
     down,
@@ -1232,11 +1321,14 @@
     w,
     small,
     idr,
+    o_block,
     o_input,
     o_dense,
     o_small,
     o_up,
     o_down,
+    yq,
+    yu,
     gu,
     gd,
     d_res,
@@ -1263,6 +1355,7 @@
     szs,
     rz,
     rzs,
+    block,
     send_sems,
     recv_sems,
     local_sems,
@@ -1299,6 +1392,59 @@
         dd = lax.rem(d + k, nd)
         wire.send(r_g + 2 * (k - 1), up_of(dd), gu.at[d], (dd, z))
         wire.send(r_g + 2 * (k - 1) + 1, down_of(dd), gd.at[d], (dd, z))
+
+    fetch = pltpu.make_async_copy(y, yq, local_sems.at[2])
+    fetch.start()
+    r_up = wire.roles(MICRO * ne)
+    r_dn = wire.roles(MICRO * ne)
+    like = yq.at[0, 0]
+
+    def pass_up(mb, to):
+        wire.send(r_up + mb * ne + to, yq.at[mb, to], yu.at[mb, to], me.up)
+
+    def pass_down(mb, to):
+        slot = jnp.where(z - 1 == to, ne, to)
+        wire.send(r_dn + mb * ne + to, yq.at[mb, to], yu.at[mb, slot], me.down)
+
+    def start_sums(mb):
+        @pl.when(z == 0)
+        def _():
+            for to in range(ne - 1, 0, -1):
+                pass_up(mb, to)
+
+        @pl.when(z == ne - 1)
+        def _():
+            for to in range(ne - 1):
+                pass_down(mb, to)
+
+    def relay(mb, hop, to):
+        @pl.when(z == hop)
+        def _():
+            wire.arrive(r_up + mb * ne + to, like)
+            yq[mb, to] = (yq[mb, to].astype(f32) + yu[mb, to].astype(f32)).astype(bf16)
+            pass_up(mb, to)
+
+        @pl.when(z == ne - 1 - hop)
+        def _():
+            low = ne - 1 - to
+            wire.arrive(r_dn + mb * ne + low, like)
+            yq[mb, low] = (yq[mb, low].astype(f32) + yu[mb, low].astype(f32)).astype(bf16)
+            pass_down(mb, low)
+
+    def end_sums(mb):
+        block[...] = resid[mb] + yq[mb, z].astype(f32)
+
+        @pl.when(z > 0)
+        def _():
+            wire.arrive(r_up + mb * ne + z, like)
+            block[...] += yu[mb, z].astype(f32)
+
+        @pl.when(z < ne - 1)
+        def _():
+            wire.arrive(r_dn + mb * ne + z, like)
+            block[...] += yu[mb, ne].astype(f32)
+
+        o_block[mb] = block[...].astype(bf16)
 
     s_rows = small[...].T
     gains = [s_rows[experts + k : experts + k + 1, :] for k in range(2)]
@@ -1359,6 +1505,9 @@
             gw[3] += g_out
             gs[...] += g_router
 
+    fetch.wait()
+    for mb in range(MICRO):
+        start_sums(mb)
     scale = 1.0 / math.sqrt(HEAD_DIM)
     for mb in range(MICRO):
         ids = idr[mb]
@@ -1372,8 +1521,11 @@
         @pl.loop(0, HEADS // 2)
         def _(pair):
             at = pl.ds(pl.multiple_of(pair * 128, 128), 128)
-            query, grad = qkv[mb, 0, own, at], dm[mb, own, at]
-            key, value = qkv[mb, 1, :, at], qkv[mb, 2, :, at]
+            query, key, value = (
+                qkv[mb, part, pl.ds(pl.multiple_of(k * D + pair * 128, 128), 128)]
+                for k, part in enumerate((own, slice(None), slice(None)))
+            )
+            grad = dm[mb, own, at]
             dq = jnp.zeros((rows, 128), f32)
             for half in range(2):
                 keep = (lane < 64) if half == 0 else (lane >= 64)
@@ -1388,6 +1540,7 @@
                 dq = dq + mm(ds, k)
             dp[0, :, at] = (dq * scale).astype(bf16)
 
+        relay(mb, 1, 3)
         wire.arrive(r_h + 4 * mb, hp.at[mb])
         wire.arrive(r_h + 4 * mb + 1, stat_src.at[mb])
         wire.arrive(r_h + 4 * mb + 2, hp.at[mb])
@@ -1404,8 +1557,11 @@
         @pl.loop(0, HEADS // 2)
         def _(pair):
             at = pl.ds(pl.multiple_of(pair * 128, 128), 128)
-            query, grad = qkv[mb, 0, :, at], dm[mb, :, at]
-            key, value = qkv[mb, 1, own, at], qkv[mb, 2, own, at]
+            query, key, value = (
+                qkv[mb, part, pl.ds(pl.multiple_of(k * D + pair * 128, 128), 128)]
+                for k, part in enumerate((slice(None), own, own))
+            )
+            grad = dm[mb, :, at]
             dk = jnp.zeros((rows, 128), f32)
             dv = jnp.zeros((rows, 128), f32)
             for half in range(2):
@@ -1422,6 +1578,8 @@
             dp[1, :, at] = (dk * scale).astype(bf16)
             dp[2, :, at] = dv.astype(bf16)
 
+        relay(mb, 2, 3)
+        relay(mb, 1, 2)
         token = tok[mb].astype(f32)
         n1t = normed(token, gains[0], s_rows[experts + 2 : experts + 3, :]).astype(bf16).T
         dn1 = jnp.zeros((rows, D), f32)
@@ -1496,6 +1654,8 @@
         o_up[x] = sum(gu[2 * k + x].astype(f32) for k in range(chips))
         o_down[x] = sum(gd[2 * k + x].astype(f32) for k in range(chips)).T
 
+    for mb in range(MICRO):
+        end_sums(mb)
     at = pl.ds(pl.multiple_of(z * share, 16), share)
     for k in range(1, ne):
         wire.arrive(r_z + 2 * (k - 1), rz.at[k])
@@ -1508,6 +1668,18 @@
         wire.left(r_g + 2 * (k - 1), gu.at[0])
         wire.left(r_g + 2 * (k - 1) + 1, gd.at[0])
     for mb in range(MICRO):
+        for to in range(1, ne):
+
+            @pl.when(z < to)
+            def _():
+                wire.left(r_up + mb * ne + to, like)
+
+        for to in range(ne - 1):
+
+            @pl.when(z > to)
+            def _():
+                wire.left(r_dn + mb * ne + to, like)
+
         for k in range(2):
             wire.left(r_h + 4 * mb + 2 * k, hp.at[0])
             wire.left(r_h + 4 * mb + 2 * k + 1, stat_src.at[0])
@@ -1523,7 +1695,7 @@
     assert wire.used <= BACK_ROLES
 
 
-BACK_ROLES = 64
+BACK_ROLES = 80
 
 
 def back(nd, ne, *args):
@@ -1536,6 +1708,7 @@
     shape = jax.ShapeDtypeStruct
     outs = (
         shape((MICRO, rows, D), bf16),
+        shape((MICRO, rows, D), bf16),
         shape((4, share, D), f32),
         shape((share, 128), f32),
         shape((2, D // nd, FF), f32),
@@ -1546,9 +1719,11 @@
     return pl.pallas_call(
         functools.partial(back_kernel, nd, ne),
         out_shape=outs,
-        in_specs=[anywhere if k in (4, 5) else vmem for k in range(len(args))],
+        in_specs=[anywhere if k in (3, 5, 6) else vmem for k in range(len(args))],
         out_specs=[vmem] * len(outs),
         scratch_shapes=[
+            v((MICRO, ne, rows, D), bf16),
+            v((MICRO, ne + 1, rows, D), bf16),
             v((nd, D // nd, FF), bf16),
             v((nd, D, FF // nd), bf16),
             v((MICRO, rows, D), f32),
@@ -1575,9 +1750,10 @@
             v((ne, share, 128), f32),
             v((ne, 4, share, D), bf16),
             v((ne, share, 128), f32),
+            v((rows, D), f32),
             pltpu.SemaphoreType.DMA((BACK_ROLES,)),
             pltpu.SemaphoreType.DMA((BACK_ROLES,)),
-            pltpu.SemaphoreType.DMA((2,)),
+            pltpu.SemaphoreType.DMA((3,)),
         ],
         compiler_params=pltpu.CompilerParams(
             collective_id=1, has_side_effects=True, vmem_limit_bytes=VMEM_BYTES
@@ -1602,12 +1778,22 @@
     cotangent,
 ):
     experts = 2 * ne
-    small = jnp.concatenate([router_weight, norm_gains.T, norm_biases.T], axis=1)
-    small = jnp.pad(small, ((0, 0), (0, 128 - experts - 4)))
-    block_out, *saved = front(
-        nd, ne, tokens, image_ids, routes, qkv_weight, out_weight, small, expert_in, expert_out, cotangent
-    )
-    input_grad, dense, small, grad_up, grad_down = back(nd, ne, tokens, cotangent, *saved)
+    saved = front(
+        nd,
+        ne,
+        tokens,
+        image_ids,
+        routes.transpose(0, 2, 1),
+        qkv_weight,
+        out_weight,
+        router_weight.T,
+        norm_gains,
+        norm_biases,
+        expert_in,
+        expert_out,
+        cotangent,
+    )
+    block_out, input_grad, dense, small, grad_up, grad_down = back(nd, ne, tokens, cotangent, *saved)
     return (
         block_out,
         input_grad,
@@ -1624,6 +1810,7 @@
 def chosen_body(nd, ne, tokens, *rest):
     rows, experts = tokens.shape[1], 2 * ne
     whole = D % (16 * nd * ne) == 0 and nd % 2 == 0 and 8 * rows == experts * rows and rows % 128 == 0
+    whole = whole and nd == 8 and ne == 4
     if whole and rest[-3].shape[0] == 2:
         return kernel_body(nd, ne, tokens, *rest)
     return body(tokens, *rest)

time: 335 us -> 263 us (0.79)
  Pallas kernels: 318 us -> 249 us
    pallas_call x1, Pallas kernels: 240 us -> 162 us  [front(): pl.pallas_call(functools.partial(front_kernel, nd, ne), out_shape=[shape(...]
    pallas_call x1, Pallas kernels: 78 us -> 87.5 us  [back(): pl.pallas_call(functools.partial(back_kernel, nd, ne), out_shape=outs, in...]
    unnamed x17 -> x11, local copies, waits for them, and re-layouts: 11.1 us -> 8.49 us
where the time goes in v1:
time: 263 us; the launch traced here: 262 us
  Pallas kernels  249 us (95%)
  local copies, waits for them, and re-layouts  12.2 us (5%)
    pallas_call x1, Pallas kernels, front(): pl.pallas_call(functools.partial(front_kernel, nd, ne), out_shape=[shape(...  162 us
    pallas_call x1, Pallas kernels, back(): pl.pallas_call(functools.partial(back_kernel, nd, ne), out_shape=outs, in...  87.5 us
    unnamed x11, local copies, waits for them, and re-layouts  8.49 us

profile of v1, /device:TPU:0, one launch (start us, length us, event | category | flops | bytes accessed | tf_op | source)
XLA Modules:
  0.0 262.2 jit_solution(6154447395166033894)
XLA Ops:
  0.6 161.7 %front.1 = (f32[2,256,512]{2,1,0:T(8,128)}, bf16[2,4,256,512]{3,2,1,0:T(8,128)(2,1)}, f32[2,256,128]{2,1,0:T(8,128)}, bf16[512,2048]{1,0:T(8,128)(2,1)}, bf16[51...) custom-call(bf16[2,256,512]{2,1,0:T(8,128)(2,1)} %tok.3, ...), custom_call_target="tpu_custom_call" | custom-call | tf_op jit(solution)/shard_map/front/pallas_call | solution.py:1251
  162.3 87.5 %back.1 = (bf16[2,256,512]{2,1,0:T(8,128)(2,1)}, bf16[2,256,512]{2,1,0:T(8,128)(2,1)}, f32[4,16,512]{2,1,0:T(8,128)}, f32[16,128]{1,0:T(8,128)}, f32[2,64,2048]{2,1,0:T(8,128)}, /*index=5*/f32[2,256,512]{2,1,0:T(8,128)}) custom-call(bf16[2,256,512]{2,1,0:T(8,128)(2,1)} %tok.3, bf16[2,256,512]{2,1,0:T(8,128)(2,1)} %cot.3, ...), custom_call_target="tpu_custom_call" | custom-call | tf_op jit(solution)/shard_map/back/pallas_call | solution.py:1719
  249.9 0.0 copy-start.1
  249.9 1.4 copy.20
  251.4 0.8 slice_bitcast_fusion.1
  252.2 0.6 copy.22
  252.8 0.6 copy.21
  253.5 1.4 slice_bitcast_fusion
  254.8 1.5 slice.15
  256.4 0.0 copy-start
  256.4 2.0 copy.27
  258.3 1.9 copy.28
  260.2 0.0 copy-done.1
  260.2 1.0 copy.29
  261.2 0.0 copy-done
  261.2 1.0 copy.30
Async XLA Ops:
  249.9 10.3 %copy-start.1 = (f32[2,64,2048]{2,1,0:T(8,128)S(1)}, f32[2,64,2048]{2,1,0:T(8,128)}, u32[]{:S(2)}) copy-start(f32[2,64,2048]{2,1,0:T(8,128)} %get-tuple-element.76) | copy-start | bytes 3145732
  256.4 4.8 %copy-start = (f32[2,256,512]{2,1,0:T(8,128)S(1)}, f32[2,256,512]{2,1,0:T(8,128)}, u32[]{:S(2)}) copy-start(f32[2,256,512]{2,1,0:T(8,128)} %get-tuple-element.77) | copy-start | bytes 3145732
